TPU v7x, 32 devices: a whole 2x2x4 slice. The times are simulated.
32 devices in a mesh: row: 16 (over z, x, core), grp: 2 (over y).
Axes of the slice: x: 2, y: 2, z: 4, core: 2. Of those that a mesh axis runs over, the one named last changes fastest.
Arguments:
- panel_rows: bfloat16 [16384, 1024], P(('row', 'grp')), may hold values from -300 to 300, as said below
- sign_bits: int32 [16384], P(('row', 'grp')), may hold values from 0 to 1
- sample_rows: int32 [8192], replicated, may hold values from 0 to 16383, as said below
Outputs:
- factor: float32 [1024, 1024], P('row', 'grp')
Inputs may be any that keep to these rules, and one draw needn't show every extreme that they name: `sample_rows`: distinct and ascending. Each aligned block of 512 rows (the rows of one device) holds at most 512 sampled rows, and at least a quarter of these blocks hold exactly 512. `panel_rows`: finite values.
All inputs are finite; a program needn't handle non-finite values.
Results may differ from a plain program's by a relative error of at most 0.0011.
Values may be sent and summed in bfloat16 or wider, within the bound.
No kernel may reach another device: no remote copies, remote signals or barrier semaphores. Data moves between devices by JAX's collectives and lax.ppermute only.
A program may use at most 64 MiB of HBM per device.

v0:
```python
import math

import jax
import jax.numpy as jnp
from jax import lax
from jax.sharding import PartitionSpec as P


def hadamard(table_size, dtype):
    row_ids = lax.broadcasted_iota(jnp.int32, (table_size, table_size), 0)
    col_ids = lax.broadcasted_iota(jnp.int32, (table_size, table_size), 1)
    shared = row_ids & col_ids
    parity = jnp.zeros((table_size, table_size), jnp.int32)
    for bit_pos in range(table_size.bit_length() - 1):
        parity = parity ^ shared >> bit_pos & 1
    return (1 - 2 * parity).astype(dtype)


def mix_lead(exchanged):
    lead_table = hadamard(exchanged.shape[0], jnp.float32)
    return jnp.einsum("ab,bic->aic", lead_table, exchanged, precision=lax.Precision.HIGHEST)


def mix_grp(exchanged):
    return lax.all_to_all(mix_lead(exchanged), "grp", split_axis=0, concat_axis=2, tiled=True)


def local(panel_rows, sign_bits, sample_rows):
    rows_dev, n_cols = panel_rows.shape
    n_row = lax.axis_size("row")
    n_grp = lax.axis_size("grp")
    flipped = panel_rows * (1 - 2 * sign_bits).astype(jnp.bfloat16)[:, None]
    local_table = hadamard(rows_dev, jnp.bfloat16)
    local_mix = jnp.dot(local_table, flipped, preferred_element_type=jnp.float32)
    grp_mixed = mix_grp(
        lax.all_to_all(local_mix[None], "grp", split_axis=2, concat_axis=0, tiled=True)
    )
    num_samples = sample_rows.shape[0]
    total_rows = rows_dev * n_row * n_grp
    norm_scale = 1.0 / math.sqrt(total_rows * num_samples)
    col_width = n_cols // n_grp
    col_start = lax.axis_index("grp") * col_width
    held = mix_lead(lax.all_to_all(grp_mixed, "row", split_axis=1, concat_axis=0, tiled=True))
    slice_width = held.shape[1]
    block_pos = lax.broadcasted_iota(jnp.int32, (n_row, slice_width), 0)
    inner_pos = lax.broadcasted_iota(jnp.int32, (n_row, slice_width), 1)
    held_ids = (
        (block_pos * n_grp + lax.axis_index("grp")) * rows_dev
        + lax.axis_index("row") * slice_width
        + inner_pos
    ).reshape(-1)
    found_pos = jnp.clip(jnp.searchsorted(sample_rows, held_ids), 0, num_samples - 1)
    is_sampled = jnp.take(sample_rows, found_pos) == held_ids
    held_flat = held.reshape(n_row * slice_width, n_cols)
    sketch_held = jnp.where(is_sampled[:, None], held_flat * norm_scale, 0.0).astype(jnp.bfloat16)
    shard_rows = lax.all_gather(sketch_held, "grp", axis=0, tiled=True)
    own_cols = lax.dynamic_slice_in_dim(shard_rows, col_start, col_width, 1)
    partial_value = lax.dot_general(
        shard_rows, own_cols, (((0,), (0,)), ((), ())), preferred_element_type=jnp.float32
    )
    gram_block = lax.psum_scatter(partial_value, "row", scatter_dimension=0, tiled=True)
    gathered = lax.all_gather(gram_block[None], ("row", "grp"), axis=0, tiled=True)
    gram_matrix = (
        gathered.reshape(n_row, n_grp, n_cols // n_row, col_width)
        .transpose(0, 2, 1, 3)
        .reshape(n_cols, n_cols)
    )
    lower_factor = jnp.linalg.cholesky(gram_matrix)
    row_width = n_cols // n_row
    return lax.dynamic_slice(
        lower_factor, (lax.axis_index("row") * row_width, col_start), (row_width, col_width)
    )


def solution(mesh):
    return jax.shard_map(
        local,
        mesh=mesh,
        in_specs=(P(("row", "grp"), None), P(("row", "grp")), P()),
        out_specs=P("row", "grp"),
        check_vma=False,
    )
```

profile of v0, /device:TPU:0, one launch (start us, length us, event | category | flops | bytes accessed | tf_op | source)
XLA Modules:
  0.0 551.8 jit_solution(12056221303512903881)
XLA Ops:
  16.0 28.9 %all_to_all.48 = f32[1,512,1024]{1,0,2:T(1,128)S(1)} all-to-all(f32[1,512,1024]{1,0,2:T(1,128)S(1)} %copy.17), channel_id=1, replica_groups=mesh['row'=16,'grp'=2] {'grp'}, dimensions={2} | all-to-all | bytes 4194304 | tf_op jit(solution)/shard_map/all_to_all | solution.py:36
  47.6 8.8 %fusion.3 = f32[2,512,512]{2,0,1:T(2,128)S(1)} fusion(f32[1,512,2,512]{3,2,1,0:T(2,128)} %copy.26), kind=kOutput, calls=%fused_computation.10 | convolution fusion | flops 12582936 | bytes 4194304 | tf_op jit(solution)/shard_map/ab,bic->aic/dot_general | solution.py:21
  62.0 23.9 %all-to-all-done.1 = f32[2,512,512]{2,1,0:T(8,128)S(1)} async-done(((f32[2,512,512]{2,1,0:T(8,128)}), f32[2,512,512]{2,1,0:T(8,128)S(1)}, u32[]{:S(2)}, u32[]{:S(2)}) %all-to-all-start.1) | async-done | bytes 2097184 | tf_op jit(solution)/shard_map/all_to_all | solution.py:25
  87.7 6.1 %copy.21 = f32[1,512,1024]{2,0,1:T(1,128)} copy(f32[1,512,1024]{1,2,0:T(8,128)} %bitcast.76) | data formatting | bytes 4194304 | tf_op jit(solution)/shard_map/all_to_all | solution.py:25
  93.8 6.4 %all-to-all-start.2 = ((f32[1,512,1024]{2,0,1:T(1,128)}), f32[1,512,1024]{2,0,1:T(1,128)S(1)}, u32[]{:S(2)}, u32[]{:S(2)}) async-start(f32[1,512,1024]{2,0,1:T(1,128)} %copy.21), calls=%async_computation.2 | async-start | bytes 4194304 | tf_op jit(solution)/shard_map/all_to_all | solution.py:43
  100.4 47.4 %while.24 = (s32[]{:T(128)}, u32[512]{0:T(512)S(1)}, u32[512]{0:T(512)S(1)}, s32[8192]{0:T(1024)S(1)}, s32[16]{0:T(128)S(1)}, /*index=5*/s32[]{:T(128)}, s32[]{:T(128)}, s32[]{}) while((s32[]{:T(128)}, u32[512]{0:T(512)S(1)}, u32[512]{0:T(512)S(1)}, s32[8192]{0:T(1024)S(1)}, s32[16]{0:T(128)S(1)}, /*index=5*/s32[]{:T(128)}, ...), condition=%wide.region_1.2_spmd.clone, body=%wide.region_0.1_spmd.clone.sunk | while | flops 10756 | bytes 46253 | solution.py:52
  156.4 33.6 %all-gather.4.cloned.1.call-done = bf16[1024,1024]{1,0:T(8,128)(2,1)} async-done(((bf16[512,1024]{1,0:T(8,128)(2,1)}), bf16[1024,1024]{1,0:T(8,128)(2,1)}) %all-gather.4.cloned.1.call-update) | async-done | bytes 2097168 | tf_op jit(solution)/shard_map/all_gather | solution.py:56
  194.6 61.9 %reduce-scatter.2.cloned.1.call-done = f32[64,512]{1,0:T(8,128)} async-done(((f32[1024,512]{1,0:T(8,128)}), f32[64,512]{1,0:T(8,128)}) %reduce-scatter.2.cloned.1.call-update) | async-done | bytes 131088 | tf_op jit(solution)/shard_map/reduce_scatter | solution.py:61
  256.6 63.5 %all-gather.6.cloned.1.call-done = f32[2048,512]{1,0:T(8,128)} async-done(((f32[64,512]{1,0:T(8,128)}), f32[2048,512]{1,0:T(8,128)}) %all-gather.6.cloned.1.call-update) | async-done | bytes 4194320 | tf_op jit(solution)/shard_map/all_gather | solution.py:62
  340.4 11.7 %cholesky.223 = f32[128,128]{1,0:T(8,128)S(1)} custom-call(f32[128,128]{1,0:T(8,128)S(1)} %cholesky.580), custom_call_target="Cholesky" | custom-call | tf_op jit(solution)/shard_map/jit(cholesky)/cholesky | solution.py:68
  352.1 9.8 %custom-call.59 = f32[1,128,128]{1,2,0:T(8,128)S(1)} custom-call(f32[1,128,128]{2,1,0:T(8,128)S(1)} %get-tuple-element.125), custom_call_target="InvertDiagBlocksLowerTriangular" | custom-call | tf_op jit(solution)/shard_map/jit(cholesky)/cholesky | solution.py:68
  368.4 12.1 %cholesky.244 = f32[128,128]{1,0:T(8,128)S(1)} custom-call(f32[128,128]{1,0:T(8,128)S(1)} %cholesky.584), custom_call_target="Cholesky" | custom-call | tf_op jit(solution)/shard_map/jit(cholesky)/cholesky | solution.py:68
  381.1 9.8 %custom-call.60 = f32[1,128,128]{1,2,0:T(8,128)S(1)} custom-call(f32[1,128,128]{2,1,0:T(8,128)S(1)} %get-tuple-element.122), custom_call_target="InvertDiagBlocksLowerTriangular" | custom-call | tf_op jit(solution)/shard_map/jit(cholesky)/cholesky | solution.py:68
  394.3 11.7 %cholesky.468 = f32[128,128]{1,0:T(8,128)S(1)} custom-call(f32[128,128]{1,0:T(8,128)S(1)} %cholesky.589), custom_call_target="Cholesky" | custom-call | tf_op jit(solution)/shard_map/jit(cholesky)/cholesky | solution.py:68
  407.2 9.8 %custom-call.61 = f32[1,128,128]{1,2,0:T(8,128)S(1)} custom-call(f32[1,128,128]{2,1,0:T(8,128)S(1)} %get-tuple-element.119), custom_call_target="InvertDiagBlocksLowerTriangular" | custom-call | tf_op jit(solution)/shard_map/jit(cholesky)/cholesky | solution.py:68
  420.6 11.8 %cholesky.487 = f32[128,128]{1,0:T(8,128)S(1)} custom-call(f32[128,128]{1,0:T(8,128)S(1)} %cholesky.594), custom_call_target="Cholesky" | custom-call | tf_op jit(solution)/shard_map/jit(cholesky)/cholesky | solution.py:68
  433.7 9.8 %custom-call.62 = f32[1,128,128]{1,2,0:T(8,128)S(1)} custom-call(f32[1,128,128]{2,1,0:T(8,128)S(1)} %get-tuple-element.116), custom_call_target="InvertDiagBlocksLowerTriangular" | custom-call | tf_op jit(solution)/shard_map/jit(cholesky)/cholesky | solution.py:68
  447.0 11.7 %cholesky.506 = f32[128,128]{1,0:T(8,128)S(1)} custom-call(f32[128,128]{1,0:T(8,128)S(1)} %cholesky.599), custom_call_target="Cholesky" | custom-call | tf_op jit(solution)/shard_map/jit(cholesky)/cholesky | solution.py:68
  460.0 10.0 %custom-call.63 = f32[1,128,128]{1,2,0:T(8,128)S(1)} custom-call(f32[1,128,128]{2,1,0:T(8,128)S(1)} %get-tuple-element.113), custom_call_target="InvertDiagBlocksLowerTriangular" | custom-call | tf_op jit(solution)/shard_map/jit(cholesky)/cholesky | solution.py:68
  473.3 11.7 %cholesky.526 = f32[128,128]{1,0:T(8,128)S(1)} custom-call(f32[128,128]{1,0:T(8,128)S(1)} %cholesky.604), custom_call_target="Cholesky" | custom-call | tf_op jit(solution)/shard_map/jit(cholesky)/cholesky | solution.py:68
  486.3 9.8 %custom-call.64 = f32[1,128,128]{1,2,0:T(8,128)S(1)} custom-call(f32[1,128,128]{2,1,0:T(8,128)S(1)} %get-tuple-element.110), custom_call_target="InvertDiagBlocksLowerTriangular" | custom-call | tf_op jit(solution)/shard_map/jit(cholesky)/cholesky | solution.py:68
  499.1 11.9 %cholesky.546 = f32[128,128]{1,0:T(8,128)S(1)} custom-call(f32[128,128]{1,0:T(8,128)S(1)} %cholesky.609), custom_call_target="Cholesky" | custom-call | tf_op jit(solution)/shard_map/jit(cholesky)/cholesky | solution.py:68
  512.3 9.8 %custom-call.65 = f32[1,128,128]{1,2,0:T(8,128)S(1)} custom-call(f32[1,128,128]{2,1,0:T(8,128)S(1)} %get-tuple-element.107), custom_call_target="InvertDiagBlocksLowerTriangular" | custom-call | tf_op jit(solution)/shard_map/jit(cholesky)/cholesky | solution.py:68
  524.7 11.7 %cholesky.564 = f32[128,128]{1,0:T(8,128)S(1)} custom-call(f32[128,128]{1,0:T(8,128)S(1)} %convolution_subtract_fusion.6), custom_call_target="Cholesky" | custom-call | tf_op jit(solution)/shard_map/jit(cholesky)/cholesky | solution.py:68
  (187 shorter events, 136.0 us)
Async XLA Ops:
  58.1 27.7 %all-to-all-start.1 = ((f32[2,512,512]{2,1,0:T(8,128)}), f32[2,512,512]{2,1,0:T(8,128)S(1)}, u32[]{:S(2)}, u32[]{:S(2)}) async-start(f32[2,512,512]{2,1,0:T(8,128)} %copy.19), calls=%async_computation.1 | async-start | bytes 4194304 | tf_op jit(solution)/shard_map/all_to_all | solution.py:25
  87.7 12.7 %copy-start = (s32[8192]{0:T(1024)S(1)}, s32[8192]{0:T(1024)}, u32[]{:S(2)}) copy-start(s32[8192]{0:T(1024)} %param.7) | copy-start | bytes 98308
  93.8 57.3 %all-to-all-start.2 = ((f32[1,512,1024]{2,0,1:T(1,128)}), f32[1,512,1024]{2,0,1:T(1,128)S(1)}, u32[]{:S(2)}, u32[]{:S(2)}) async-start(f32[1,512,1024]{2,0,1:T(1,128)} %copy.21), calls=%async_computation.2 | async-start | bytes 4194304 | tf_op jit(solution)/shard_map/all_to_all | solution.py:43
  100.2 89.8 %all-gather.4.cloned.1.call-start = ((), (), s32[]{:S(2)}) async-start(), calls=%async_computation.4 | async-start | bytes 3145728 | tf_op jit(solution)/shard_map/all_gather | solution.py:56
  156.3 100.2 %reduce-scatter.2.cloned.1.call-start = ((), (), s32[]{:S(2)}) async-start(), calls=%async_computation.5 | async-start | bytes 2228224 | tf_op jit(solution)/shard_map/reduce_scatter | solution.py:61
  194.5 125.5 %all-gather.6.cloned.1.call-start = ((), (), s32[]{:S(2)}) async-start(), calls=%async_computation.6 | async-start | bytes 4325376 | tf_op jit(solution)/shard_map/all_gather | solution.py:62
  338.4 1.9 copy-start.1
Sparse Core Ops, SparseCore 0:
  156.5 33.4 all-gather.3
  194.7 61.8 reduce-scatter.1
  259.4 60.5 all-gather.5
where the time goes:
time: 558 us; the launch traced here: 552 us
  waiting for transfers between devices  183 us (33%)
  other arithmetic  182 us (33%)
  local copies, waits for them, and re-layouts  84.7 us (15%)
  matrix products  43.4 us (8%)
  blocking collectives  28.9 us (5%)
  between operations  18.7 us (3%)
  starting transfers between devices  10.4 us (2%)
    another operation x30, other arithmetic, local(): lower_factor = jnp.linalg.cholesky(gram_matrix)  172 us
    all_gather x1, waiting for transfers between devices, local(): lax.all_gather(gram_block[None], ('row', 'grp'), axis=0, tiled=True)  63.5 us
    reduce_scatter x1, waiting for transfers between devices, local(): lax.psum_scatter(partial_value, 'row', scatter_dimension=0, tiled=True)  61.9 us
    gather x14, local copies, waits for them, and re-layouts, local(): jnp.searchsorted(sample_rows, held_ids)  44 us
    all_gather x1, waiting for transfers between devices, local(): shard_rows = lax.all_gather(sketch_held, 'grp', axis=0, tiled=True)  33.6 us
    all_to_all x1, blocking collectives, local(): lax.all_to_all(local_mix[None], 'grp', split_axis=2, concat_axis=0, tiled...  28.9 us
    all_to_all x1, waiting for transfers between devices, mix_grp(): lax.all_to_all(mix_lead(exchanged), 'grp', split_axis=0, concat_axis=2, t...  23.9 us
    another operation x14, matrix products, local(): lower_factor = jnp.linalg.cholesky(gram_matrix)  23.1 us
  transfers between devices with their start and end apart: 5, of which 4 were waited for; matrix products, arithmetic and copies ran while one was open for 9% of the time, Pallas kernels for 0%

commit v1 on v0

--- a/solution.py
+++ b/solution.py
@@ -1,9 +1,17 @@
+import functools
 import math
 
 import jax
 import jax.numpy as jnp
 from jax import lax
+from jax.experimental import pallas as pl
+from jax.experimental.pallas import tpu as pltpu
 from jax.sharding import PartitionSpec as P
+
+AXES = ("row", "grp")
+TILE = 128
+f32 = jnp.float32
+HI = lax.Precision.HIGHEST
 
 
 def hadamard(table_size, dtype):
@@ -25,7 +33,7 @@
     return lax.all_to_all(mix_lead(exchanged), "grp", split_axis=0, concat_axis=2, tiled=True)
 
 
-def local(panel_rows, sign_bits, sample_rows):
+def local_plain(panel_rows, sign_bits, sample_rows):
     rows_dev, n_cols = panel_rows.shape
     n_row = lax.axis_size("row")
     n_grp = lax.axis_size("grp")
@@ -72,6 +80,314 @@
     )
 
 
+def mm(a,b,dims=(((1,),(0,)),((),()))):
+    return lax.dot_general(a,b,dims,precision=HI,preferred_element_type=f32)
+TA=(((0,),(0,)),((),()))
+TB=(((1,),(1,)),((),()))
+
+def elim(X, sbase, ibase, n, zero=None):
+    G=n//8
+    xs=[X[8*g:8*g+8,:] for g in range(G)]
+    rid=lax.broadcasted_iota(jnp.int32,(8,128),0)
+    full=lambda v: jnp.broadcast_to(v,(8,128))
+    out=[]
+    for g in range(G):
+        C=[[None]*G for _ in range(8)]
+        for m in range(8):
+            for h in range(g,G):
+                l=sbase+8*g+m
+                C[m][h]=full(xs[h][:,l:l+1])
+        for m in range(8): C[m][g]=C[m][g]+zero
+        o=jnp.zeros((8,128),f32)
+        for j in range(0,8,2):
+            a=full(C[j][g][j:j+1,:]); b=full(C[j][g][j+1:j+2,:]); c=full(C[j+1][g][j+1:j+2,:])
+            r0=full(xs[g][j:j+1,:]); r1=full(xs[g][j+1:j+2,:])
+            det=a*c-b*b
+            inv=1.0/det
+            ws=[]
+            for m in range(j+2,8):
+                q0=full(C[m][g][j:j+1,:]); q1=full(C[m][g][j+1:j+2,:])
+                if j==0:
+                    q0=q0; q1=q1
+                ws.append((m,(c*q0-b*q1)*inv,(a*q1-b*q0)*inv))
+            t1=a*r1-b*r0
+            u0=(c*r0-b*r1)*inv; u1=t1*inv
+            for m,w0,w1 in ws:
+                for h in range(g,G):
+                    C[m][h]=C[m][h]-C[j][h]*w0-C[j+1][h]*w1
+            for h in range(g,G):
+                if h>g or j<6:
+                    xs[h]=xs[h]-C[j][h]*u0-C[j+1][h]*u1
+            l0=r0*lax.rsqrt(a); l1=t1*lax.rsqrt(a*det)
+            o=jnp.where(rid==j,l0,jnp.where(rid==j+1,l1,o))
+        out.append(o)
+    return jnp.concatenate(out,axis=0)
+
+def factor128(D,zero):
+    lane=lax.broadcasted_iota(jnp.int32,(64,128),1)
+    row=lax.broadcasted_iota(jnp.int32,(64,128),0)
+    z=jnp.zeros((64,128),f32)
+    def equil(S,off,ioff):
+        e=lane==row+off
+        dg=jnp.where(e,S,0.0)
+        dc=lax.rsqrt(jnp.sum(dg,axis=1,keepdims=True))
+        dsum=jnp.sum(dg,axis=0,keepdims=True)
+        half=(lane>=off)&(lane<off+64)
+        drow=jnp.where(half[0:1],dsum,1.0)
+        dr=lax.rsqrt(drow)
+        X=jnp.where(half,S*dc*dr,jnp.where(lane==row+ioff,dc,0.0))
+        back=jnp.where(half[0:1],drow*dr,1.0)
+        return X,back
+    Dt=D[:64,:]; Db=D[64:,:]
+    X1,bk1=equil(Dt,0,64)
+    F1=elim(X1,0,64,64,zero)*bk1
+    U1=mm(F1,jnp.concatenate([z,Dt],axis=0))
+    U12=jnp.where(lane>=64,U1,0.0)
+    T=mm(U12,U12,TA)
+    D2=Db-T[64:,:]
+    X2,bk2=equil(D2,64,0)
+    F2=elim(X2,64,0,64,zero)*bk2
+    W1=jnp.where(lane>=64,F1,0.0)
+    Q=mm(U12,F1,TA)
+    V=mm(F2,jnp.concatenate([Q[64:,:],z],axis=0))
+    W1s=pltpu.roll(F1,64,1); Vs=pltpu.roll(V,64,1)
+    lo=lane<64
+    Wtop=jnp.where(lo,W1s,0.0)
+    W2s=pltpu.roll(F2,64,1)
+    Wbot=jnp.where(lo,-Vs,W2s)
+    Utop=jnp.where(lo,jnp.where(lane>=row,F1,0.0),U1)
+    Ubot=jnp.where((~lo)&(lane-64>=row),F2,0.0)
+    return jnp.concatenate([Utop,Ubot],axis=0),jnp.concatenate([Wtop,Wbot],axis=0)
+
+
+def sketch_gram_kernel(n_dev, me_ref, x_ref, m_ref, keep_ref, send_ref, s_ref, fold):
+    n = x_ref.shape[2]
+    nb = n // TILE
+    per = x_ref.shape[1]
+
+    def mix(c, _):
+        cols = pl.ds(pl.multiple_of(c * TILE, TILE), TILE)
+        for sub in range(per // 8):
+            v = [x_ref[b, 8 * sub : 8 * sub + 8, cols] for b in range(n_dev)]
+            h = 1
+            while h < n_dev:
+                w = list(v)
+                for b in range(n_dev):
+                    if not b & h:
+                        w[b] = v[b] + v[b | h]
+                        w[b | h] = v[b] - v[b | h]
+                v = w
+                h *= 2
+            for b in range(0, n_dev, 2):
+                r = (sub * n_dev + b) * 8
+                pair = jnp.concatenate([v[b], v[b + 1]], axis=0) * m_ref[r : r + 16, :]
+                s_ref[r : r + 16, cols] = pair.astype(jnp.bfloat16)
+        return 0
+
+    lax.fori_loop(0, nb, mix, 0)
+    for k in range(nb):
+        part = lax.dot_general(
+            s_ref[:, k * TILE : (k + 1) * TILE],
+            s_ref[:, k * TILE :],
+            TA,
+            preferred_element_type=f32,
+        )
+        panel, off = (k, 0) if k < nb // 2 else (nb - 1 - k, k + 1)
+        fold[panel * TILE : (panel + 1) * TILE, off * TILE : (off + nb - k) * TILE] = part
+    half = n_dev // 2
+    me = me_ref[0]
+    h = keep_ref.shape[1]
+
+    def put(j, _):
+        keep_ref[j] = fold[pl.ds(pl.multiple_of((j ^ me) * h, 8), h), :]
+        send_ref[j] = fold[pl.ds(pl.multiple_of(((j + half) ^ me) * h, 8), h), :]
+        return 0
+
+    lax.fori_loop(0, half, put, 0)
+
+
+def factor_kernel(n, pos_ref, own_ref, recv_ref, out_ref, fold, u_ref, strip, zref, turn):
+    B = TILE
+    nb = n // B
+    CW = 2 * B
+    half = own_ref.shape[0]
+    h = own_ref.shape[1]
+    me = pos_ref[0]
+
+    def get(j, _):
+        fold[pl.ds(pl.multiple_of((j ^ me) * h, 8), h), :] = own_ref[j]
+        fold[pl.ds(pl.multiple_of(((j + half) ^ me) * h, 8), h), :] = recv_ref[j]
+        return 0
+
+    lax.fori_loop(0, half, get, 0)
+    zref[...] = jnp.zeros((8, 128), f32)
+
+    def body(k, _):
+        kc = pl.multiple_of(k * B, B)
+        low = k < nb // 2
+        panel = jnp.where(low, k, nb - 1 - k)
+        off = jnp.where(low, -k, 1)
+
+        def load(c, _):
+            src = pl.multiple_of((c + off) * B, B)
+            strip[:, pl.ds(pl.multiple_of(c * B, B), B)] = fold[
+                pl.ds(pl.multiple_of(panel * B, B), B), pl.ds(src, B)
+            ]
+            return 0
+
+        lax.fori_loop(k, nb, load, 0)
+        c0 = kc // CW
+        nc = n // CW
+
+        def chunk(c, _):
+            cc = pl.multiple_of(c * CW, CW)
+
+            def kk(j, acc):
+                jj = pl.multiple_of(j * B, B)
+                return acc + mm(u_ref[pl.ds(jj, B), pl.ds(kc, B)], u_ref[pl.ds(jj, B), pl.ds(cc, CW)], TA)
+
+            acc = lax.fori_loop(0, k, kk, jnp.zeros((B, CW), f32))
+            strip[:, pl.ds(cc, CW)] = strip[:, pl.ds(cc, CW)] - acc
+            return 0
+
+        lax.fori_loop(c0, nc, chunk, 0)
+        U, W = factor128(strip[:, pl.ds(kc, B)], zref[...])
+
+        def pan(c, _):
+            cc = pl.multiple_of(c * CW, CW)
+            u_ref[pl.ds(kc, B), pl.ds(cc, CW)] = mm(W, strip[:, pl.ds(cc, CW)])
+            return 0
+
+        lax.fori_loop(c0, nc, pan, 0)
+        u_ref[pl.ds(kc, B), pl.ds(kc, B)] = U
+        return 0
+
+    lax.fori_loop(0, nb, body, 0)
+    row_width, col_width = out_ref.shape
+    first_row = pos_ref[1] * row_width
+    first_col = pos_ref[2] * col_width
+    lane_tile = pl.multiple_of(first_row // B * B, B)
+    inner = pl.multiple_of(first_row % B, 8)
+    for c in range(col_width // B):
+        block = u_ref[pl.ds(pl.multiple_of(first_col + c * B, B), B), pl.ds(lane_tile, B)]
+        turn[...] = block.T
+        i = first_row + lax.broadcasted_iota(jnp.int32, (row_width, B), 0)
+        j = first_col + c * B + lax.broadcasted_iota(jnp.int32, (row_width, B), 1)
+        out_ref[:, c * B : (c + 1) * B] = jnp.where(j <= i, turn[pl.ds(inner, row_width), :], 0.0)
+
+
+def xor_send(value, mask, n_dev):
+    return lax.ppermute(value, AXES, [(d, d ^ mask) for d in range(n_dev)])
+
+
+def local_fast(panel_rows, sign_bits, sample_rows):
+    rows_dev, n = panel_rows.shape
+    n_row = lax.axis_size("row")
+    n_grp = lax.axis_size("grp")
+    n_dev = n_row * n_grp
+    per = rows_dev // n_dev
+    num_samples = sample_rows.shape[0]
+    norm_scale = 1.0 / math.sqrt(rows_dev * n_dev * num_samples)
+    row_i = lax.axis_index("row")
+    grp_i = lax.axis_index("grp")
+    lin = row_i * n_grp + grp_i
+
+    flipped = panel_rows * (1 - 2 * sign_bits).astype(jnp.bfloat16)[:, None]
+    local_mix = jnp.dot(hadamard(rows_dev, jnp.bfloat16), flipped, preferred_element_type=f32)
+    mixed = lax.all_to_all(local_mix, AXES, split_axis=0, concat_axis=0, tiled=True)
+    mixed = mixed.reshape(n_dev, per, n)
+
+    r = lax.iota(jnp.int32, rows_dev)
+    held_ids = (r // 8 % n_dev) * rows_dev + lin * per + r // (8 * n_dev) * 8 + r % 8
+    is_sampled = jnp.any(held_ids[:, None] == sample_rows[None, :], axis=1)
+    weight = jnp.where(is_sampled, norm_scale, 0.0).astype(f32)
+    weight = jnp.broadcast_to(weight[:, None], (rows_dev, TILE))
+
+    grp_bits = [1 << b for b in range(n_grp.bit_length() - 1)]
+    row_bits = [n_grp << b for b in range(n_row.bit_length() - 1)]
+    stages = [row_bits[:1], row_bits[1:2] + grp_bits, row_bits[2:]]
+    order = [bit for stage in stages for bit in reversed(stage)]
+    place = jnp.int32(0)
+    for bit in order:
+        place = place * 2 + (lin & bit) // bit
+
+    def mask_of(stage, step):
+        return sum(bit for pos, bit in enumerate(stage) if step >> pos & 1)
+
+    nb = n // TILE
+    fold_rows = nb // 2 * TILE
+    fold_cols = (nb + 1) * TILE
+    h = fold_rows // n_dev
+    half = n_dev // 2
+    piece = jax.ShapeDtypeStruct((half, h, fold_cols), f32)
+    vmem = pl.BlockSpec(memory_space=pltpu.VMEM)
+    smem = pl.BlockSpec(memory_space=pltpu.SMEM)
+    keep, send = pl.pallas_call(
+        functools.partial(sketch_gram_kernel, n_dev),
+        out_shape=(piece, piece),
+        in_specs=[smem, vmem, vmem],
+        out_specs=(vmem, vmem),
+        scratch_shapes=[pltpu.VMEM((rows_dev, n), jnp.bfloat16), pltpu.VMEM((fold_rows, fold_cols), f32)],
+        compiler_params=pltpu.CompilerParams(vmem_limit_bytes=40 << 20),
+        name="sketch_gram",
+    )(place[None], mixed, weight)
+
+    total = keep + xor_send(send, mask_of(stages[0], 1), n_dev)
+    for stage in stages[1:]:
+        ways = 1 << len(stage)
+        if ways == 1:
+            continue
+        parts = total.reshape(ways, total.shape[0] // ways, h, fold_cols)
+        got = [xor_send(parts[s], mask_of(stage, s), n_dev) for s in range(1, ways)]
+        total = parts[0]
+        for g in got:
+            total = total + g
+    for stage in reversed(stages[1:]):
+        ways = 1 << len(stage)
+        if ways == 1:
+            continue
+        got = [xor_send(total, mask_of(stage, s), n_dev) for s in range(1, ways)]
+        total = jnp.concatenate([total] + got, axis=0)
+    other = xor_send(total, mask_of(stages[0], 1), n_dev)
+
+    row_width = n // n_row
+    col_width = n // n_grp
+    return pl.pallas_call(
+        functools.partial(factor_kernel, n),
+        out_shape=jax.ShapeDtypeStruct((row_width, col_width), f32),
+        in_specs=[smem, vmem, vmem],
+        out_specs=vmem,
+        scratch_shapes=[
+            pltpu.VMEM((fold_rows, fold_cols), f32),
+            pltpu.VMEM((n, n), f32),
+            pltpu.VMEM((TILE, n), f32),
+            pltpu.VMEM((8, 128), f32),
+            pltpu.VMEM((TILE, TILE), f32),
+        ],
+        compiler_params=pltpu.CompilerParams(vmem_limit_bytes=40 << 20),
+        name="factor",
+    )(jnp.stack([place, row_i, grp_i]), total, other)
+
+
+def local(panel_rows, sign_bits, sample_rows):
+    rows_dev, n = panel_rows.shape
+    n_row = lax.axis_size("row")
+    n_grp = lax.axis_size("grp")
+    n_dev = n_row * n_grp
+    fits = (
+        n % (2 * TILE) == 0
+        and n_dev & (n_dev - 1) == 0
+        and 2 <= n_row
+        and n_dev <= 64
+        and rows_dev % (8 * n_dev) == 0
+        and n // 2 % (8 * n_dev) == 0
+        and TILE % (n // n_row) == 0
+        and n // n_row % 8 == 0
+        and n // n_grp % TILE == 0
+    )
+    return (local_fast if fits else local_plain)(panel_rows, sign_bits, sample_rows)
+
+
 def solution(mesh):
     return jax.shard_map(
         local,

time: 558 us -> 169 us (0.30); the launches traced: 552 us -> 168 us
  other arithmetic: 182 us -> 3.32 us
  waiting for transfers between devices: 183 us -> 84.2 us
  local copies, waits for them, and re-layouts: 84.7 us -> 0.29 us
  Pallas kernels: 0 us -> 53.5 us
  matrix products: 43.4 us -> 4.16 us
  blocking collectives: 28.9 us -> 0 us
  between operations: 18.7 us -> 0.2 us
  starting transfers between devices: 10.4 us -> 22.8 us
    another operation x30 -> x1, other arithmetic: 172 us -> 0.08 us  [local_fast(): jnp.stack([place, row_i, grp_i])]
    all_gather x2 -> x0, waiting for transfers between devices: 97.1 us -> none  [the longest x1 63.5 us: local(): lax.all_gather(gram_block[None], ('row', 'grp'), axis=0, tiled=True)]
    reduce_scatter x1 -> x0, waiting for transfers between devices: 61.9 us -> none  [local(): lax.psum_scatter(partial_value, 'row', scatter_dimension=0, tiled=True)]
    pallas_call x0 -> x2, Pallas kernels: none -> 53.5 us  [the longest x1 51.7 us: local_fast(): pl.pallas_call(functools.partial(factor_kernel, n), out_shape=jax.ShapeDt...]
    gather x15 -> x0, local copies, waits for them, and re-layouts: 47.1 us -> none  [the longest x14 44 us: local(): jnp.searchsorted(sample_rows, held_ids)]
    ppermute x0 -> x14, waiting for transfers between devices: none -> 37.9 us  [xor_send(): return lax.ppermute(value, AXES, [(d, d ^ mask) for d in range(n_dev)])]
    all_to_all x1 -> x0, blocking collectives: 28.9 us -> none  [local(): lax.all_to_all(local_mix[None], 'grp', split_axis=2, concat_axis=0, tiled...]
    another operation x14 -> x0, matrix products: 23.1 us -> none  [local(): lower_factor = jnp.linalg.cholesky(gram_matrix)]
  transfers between devices with their start and end apart: 5 -> 15, of which waited for: 4 -> 12; matrix products, arithmetic and copies ran while one was open for 9% -> 1% of each run, Pallas kernels for 0% -> 0%
where the time goes in v1:
time: 169 us; the launch traced here: 168 us
  waiting for transfers between devices  84.2 us (50%)
  Pallas kernels  53.5 us (32%)
  starting transfers between devices  22.8 us (13%)
  matrix products  4.16 us (2%)
  other arithmetic  3.32 us (2%)
    pallas_call x1, Pallas kernels, local_fast(): pl.pallas_call(functools.partial(factor_kernel, n), out_shape=jax.ShapeDt...  51.7 us
    all_to_all x1, waiting for transfers between devices, local_fast(): lax.all_to_all(local_mix, AXES, split_axis=0, concat_axis=0, tiled=True)  46.3 us
    ppermute x14, waiting for transfers between devices, xor_send(): return lax.ppermute(value, AXES, [(d, d ^ mask) for d in range(n_dev)])  37.9 us
    ppermute x14, starting transfers between devices, xor_send(): return lax.ppermute(value, AXES, [(d, d ^ mask) for d in range(n_dev)])  15.4 us
    all_to_all x1, starting transfers between devices, local_fast(): lax.all_to_all(local_mix, AXES, split_axis=0, concat_axis=0, tiled=True)  7.32 us
    dot_general x1, matrix products, local_fast(): jnp.dot(hadamard(rows_dev, jnp.bfloat16), flipped, preferred_element_type...  4.16 us
  transfers between devices with their start and end apart: 15, of which 12 were waited for; matrix products, arithmetic and copies ran while one was open for 1% of the time, Pallas kernels for 0%

profile of v1, /device:TPU:0, one launch (start us, length us, event | category | flops | bytes accessed | tf_op | source)
XLA Modules:
  0.0 168.4 jit_solution(4669746590948088317)
XLA Ops:
  0.7 4.2 %fusion = f32[512,1024]{1,0:T(8,128)} fusion(bf16[512,1024]{1,0:T(8,128)(2,1)} %param.3, bf16[512]{0:T(512)(128)(2,1)S(1)} %subtract_convert_fusion.2), kind=kOutput, calls=%fused_computation.1 | convolution fusion | flops 545259520 | bytes 3146752 | tf_op jit(solution)/shard_map/dot_general | solution.py:296
  4.8 7.3 %all-to-all-start = ((f32[32,16,1024]{2,1,0:T(8,128)}), f32[32,16,1024]{2,1,0:T(8,128)S(1)}, u32[]{:S(2)}, u32[]{:S(2)}) async-start(f32[32,16,1024]{2,1,0:T(8,128)} %bitcast.4), calls=%async_computation | async-start | bytes 4194304 | tf_op jit(solution)/shard_map/all_to_all | solution.py:297
  12.3 2.3 %compare_reduce_fusion = pred[512]{0:T(512)(128)(4,1)S(1)} fusion(s32[8192]{0:T(1024)S(1)} %copy-done, s32[512]{0:T(512)S(1)} %fusion.24), kind=kLoop, calls=%fused_computation | loop fusion | flops 8388096 | bytes 35328 | tf_op jit(solution)/shard_map/reduce_or | solution.py:302
  14.5 46.3 %all-to-all-done.x_ref = f32[32,16,1024]{2,1,0:T(8,128)S(1)} async-done(((f32[32,16,1024]{2,1,0:T(8,128)}), f32[32,16,1024]{2,1,0:T(8,128)S(1)}, u32[]{:S(2)}, u32[]{:S(2)}) %all-to-all-start) | async-done | bytes 2097184 | tf_op jit(solution)/shard_map/all_to_all | solution.py:297
  61.0 1.8 %sketch_gram.1 = (f32[16,16,1152]{2,1,0:T(8,128)S(1)}, f32[16,16,1152]{2,1,0:T(8,128)S(1)}) custom-call(s32[1]{0:T(128)} %bitcast.me_ref, f32[32,16,1024]{2,1,0:T(8,128)S(1)} %all-to-all-done.x_ref, f32[512,128]{1,0:T(8,128)S(1)} %broadcast_in_dim.20.m_ref), custom_call_target="tpu_custom_call" | custom-call | tf_op jit(solution)/shard_map/sketch_gram/pallas_call | solution.py:325
  62.9 2.8 %collective-permute-done = f32[16,16,1152]{2,1,0:T(8,128)S(1)} collective-permute-done((f32[16,16,1152]{2,1,0:T(8,128)S(1)}, f32[16,16,1152]{2,1,0:T(8,128)S(1)}, u32[]{:S(2)}, u32[]{:S(2)}) %collective-permute-start) | collective-permute-done | bytes 1179680 | tf_op jit(solution)/shard_map/ppermute | solution.py:280
  65.9 1.5 collective-permute-start.1
  67.5 1.6 collective-permute-start.3
  69.5 6.4 %collective-permute-done.1 = f32[4,16,1152]{2,1,0:T(8,128)S(1)} collective-permute-done((f32[4,16,1152]{2,1,0:T(8,128)S(1)}, f32[4,16,1152]{2,1,0:T(8,128)S(1)}, u32[]{:S(2)}, u32[]{:S(2)}) %collective-permute-start.1) | collective-permute-done | bytes 294944 | tf_op jit(solution)/shard_map/ppermute | solution.py:280
  75.9 6.7 %collective-permute-done.3 = f32[4,16,1152]{2,1,0:T(8,128)S(1)} collective-permute-done((f32[4,16,1152]{2,1,0:T(8,128)S(1)}, f32[4,16,1152]{2,1,0:T(8,128)S(1)}, u32[]{:S(2)}, u32[]{:S(2)}) %collective-permute-start.3) | collective-permute-done | bytes 294944 | tf_op jit(solution)/shard_map/ppermute | solution.py:280
  82.5 1.4 collective-permute-done.2
  85.6 2.0 %collective-permute-start.5 = (f32[1,16,1152]{2,1,0:T(8,128)S(1)}, f32[1,16,1152]{2,1,0:T(8,128)S(1)}, u32[]{:S(2)}, u32[]{:S(2)}) collective-permute-start(f32[1,16,1152]{2,1,0:T(8,128)S(1)} %get-tuple-element.16), channel_id=1, source_target_pairs={{0,16},{1,17},{2,18},{3,19},{4,20},{5,21},{6,22},{7,23},{8,24},{9,... | collective-permute-start | bytes 221192 | tf_op jit(solution)/shard_map/ppermute | solution.py:280
  87.5 1.4 collective-permute-done.4
  88.9 1.8 %collective-permute-done.6 = f32[1,16,1152]{2,1,0:T(8,128)S(1)} collective-permute-done((f32[1,16,1152]{2,1,0:T(8,128)S(1)}, f32[1,16,1152]{2,1,0:T(8,128)S(1)}, u32[]{:S(2)}, u32[]{:S(2)}) %collective-permute-start.6) | collective-permute-done | bytes 73760 | tf_op jit(solution)/shard_map/ppermute | solution.py:280
  90.7 2.2 %collective-permute-done.5 = f32[1,16,1152]{2,1,0:T(8,128)S(1)} collective-permute-done((f32[1,16,1152]{2,1,0:T(8,128)S(1)}, f32[1,16,1152]{2,1,0:T(8,128)S(1)}, u32[]{:S(2)}, u32[]{:S(2)}) %collective-permute-start.5) | collective-permute-done | bytes 73760 | tf_op jit(solution)/shard_map/ppermute | solution.py:280
  93.0 2.2 %collective-permute-start.9 = (f32[1,16,1152]{2,1,0:T(8,128)S(1)}, f32[1,16,1152]{2,1,0:T(8,128)S(1)}, u32[]{:S(2)}, u32[]{:S(2)}) collective-permute-start(f32[1,16,1152]{2,1,0:T(8,128)S(1)} %get-tuple-element.10), channel_id=1, source_target_pairs={{0,24},{1,25},{2,26},{3,27},{4,28},{5,29},{6,30},{7,31},{8,16},{9,... | collective-permute-start | bytes 221192 | tf_op jit(solution)/shard_map/ppermute | solution.py:280
  95.1 2.3 %collective-permute-start.7 = (f32[1,16,1152]{2,1,0:T(8,128)S(1)}, f32[1,16,1152]{2,1,0:T(8,128)S(1)}, u32[]{:S(2)}, u32[]{:S(2)}) collective-permute-start(f32[1,16,1152]{2,1,0:T(8,128)S(1)} %get-tuple-element.10), channel_id=1, source_target_pairs={{0,8},{1,9},{2,10},{3,11},{4,12},{5,13},{6,14},{7,15},{8,0},{9,1},... | collective-permute-start | bytes 221192 | tf_op jit(solution)/shard_map/ppermute | solution.py:280
  97.4 1.8 %collective-permute-done.9 = f32[1,16,1152]{2,1,0:T(8,128)S(1)} collective-permute-done((f32[1,16,1152]{2,1,0:T(8,128)S(1)}, f32[1,16,1152]{2,1,0:T(8,128)S(1)}, u32[]{:S(2)}, u32[]{:S(2)}) %collective-permute-start.9) | collective-permute-done | bytes 73760 | tf_op jit(solution)/shard_map/ppermute | solution.py:280
  99.2 1.6 collective-permute-done.8
  100.8 1.9 %collective-permute-start.12 = (f32[4,16,1152]{2,1,0:T(8,128)S(1)}, f32[4,16,1152]{2,1,0:T(8,128)S(1)}, u32[]{:S(2)}, u32[]{:S(2)}) collective-permute-start(f32[4,16,1152]{2,1,0:T(8,128)S(1)} %pad_maximum_fusion), channel_id=1, source_target_pairs={{0,5},{1,4},{2,7},{3,6},{4,1},{5,0},{6,3},{7,2},{8,13},{9,12},{10,... | collective-permute-start | bytes 884744 | tf_op jit(solution)/shard_map/ppermute | solution.py:280
  102.7 1.8 %collective-permute-start.11 = (f32[4,16,1152]{2,1,0:T(8,128)S(1)}, f32[4,16,1152]{2,1,0:T(8,128)S(1)}, u32[]{:S(2)}, u32[]{:S(2)}) collective-permute-start(f32[4,16,1152]{2,1,0:T(8,128)S(1)} %pad_maximum_fusion), channel_id=1, source_target_pairs={{0,1},{1,0},{2,3},{3,2},{4,5},{5,4},{6,7},{7,6},{8,9},{9,8},{10,11... | collective-permute-start | bytes 884744 | tf_op jit(solution)/shard_map/ppermute | solution.py:280
  104.6 9.1 %collective-permute-done.10 = f32[4,16,1152]{2,1,0:T(8,128)S(1)} collective-permute-done((f32[4,16,1152]{2,1,0:T(8,128)S(1)}, f32[4,16,1152]{2,1,0:T(8,128)S(1)}, u32[]{:S(2)}, u32[]{:S(2)}) %collective-permute-start.10) | collective-permute-done | bytes 294944 | tf_op jit(solution)/shard_map/ppermute | solution.py:280
  113.9 2.8 %collective-permute-done.13.recv_ref = f32[16,16,1152]{2,1,0:T(8,128)S(1)} collective-permute-done((f32[16,16,1152]{2,1,0:T(8,128)S(1)}, f32[16,16,1152]{2,1,0:T(8,128)S(1)}, u32[]{:S(2)}, u32[]{:S(2)}) %collective-permute-start.13) | collective-permute-done | bytes 1179680 | tf_op jit(solution)/shard_map/ppermute | solution.py:280
  116.7 51.7 %factor.1 = f32[64,512]{1,0:T(8,128)} custom-call(s32[3]{0:T(128)S(1)} %pad_add_fusion.pos_ref, f32[16,16,1152]{2,1,0:T(8,128)S(1)} %constant_dynamic-update-slice_fusion.own_ref, f32[16,16,1152]{2,1,0:T(8,128)S(1)} %collective-permute-done.13.recv_ref), custom_call_target="tpu_custom_call" | custom-call | tf_op jit(solution)/shard_map/factor/pallas_call | solution.py:355
  (29 shorter events, 3.4 us)
Async XLA Ops:
  4.8 7.4 %copy-start = (s32[8192]{0:T(1024)S(1)}, s32[8192]{0:T(1024)}, u32[]{:S(2)}) copy-start(s32[8192]{0:T(1024)} %param.5) | copy-start | bytes 98308
  4.8 56.0 %all-to-all-start = ((f32[32,16,1024]{2,1,0:T(8,128)}), f32[32,16,1024]{2,1,0:T(8,128)S(1)}, u32[]{:S(2)}, u32[]{:S(2)}) async-start(f32[32,16,1024]{2,1,0:T(8,128)} %bitcast.4), calls=%async_computation | async-start | bytes 4194304 | tf_op jit(solution)/shard_map/all_to_all | solution.py:297
  62.8 2.9 %collective-permute-start = (f32[16,16,1152]{2,1,0:T(8,128)S(1)}, f32[16,16,1152]{2,1,0:T(8,128)S(1)}, u32[]{:S(2)}, u32[]{:S(2)}) collective-permute-start(f32[16,16,1152]{2,1,0:T(8,128)S(1)} %get-tuple-element.8), channel_id=1, source_target_pairs={{0,2},{1,3},{2,0},{3,1},{4,6},{5,7},{6,4},{7,5},{8,10},{9,11},{10,... | collective-permute-start | bytes 3538952 | tf_op jit(solution)/shard_map/ppermute | solution.py:280
  65.9 9.9 %collective-permute-start.1 = (f32[4,16,1152]{2,1,0:T(8,128)S(1)}, f32[4,16,1152]{2,1,0:T(8,128)S(1)}, u32[]{:S(2)}, u32[]{:S(2)}) collective-permute-start(f32[4,16,1152]{2,1,0:T(8,128)S(1)} %get-tuple-element.11), channel_id=1, source_target_pairs={{0,4},{1,5},{2,6},{3,7},{4,0},{5,1},{6,2},{7,3},{8,12},{9,13},{10,... | collective-permute-start | bytes 884744 | tf_op jit(solution)/shard_map/ppermute | solution.py:280
  67.5 15.1 %collective-permute-start.3 = (f32[4,16,1152]{2,1,0:T(8,128)S(1)}, f32[4,16,1152]{2,1,0:T(8,128)S(1)}, u32[]{:S(2)}, u32[]{:S(2)}) collective-permute-start(f32[4,16,1152]{2,1,0:T(8,128)S(1)} %get-tuple-element.12), channel_id=1, source_target_pairs={{0,5},{1,4},{2,7},{3,6},{4,1},{5,0},{6,3},{7,2},{8,13},{9,12},{10,... | collective-permute-start | bytes 884744 | tf_op jit(solution)/shard_map/ppermute | solution.py:280
  69.1 14.8 %collective-permute-start.2 = (f32[4,16,1152]{2,1,0:T(8,128)S(1)}, f32[4,16,1152]{2,1,0:T(8,128)S(1)}, u32[]{:S(2)}, u32[]{:S(2)}) collective-permute-start(f32[4,16,1152]{2,1,0:T(8,128)S(1)} %get-tuple-element.13), channel_id=1, source_target_pairs={{0,1},{1,0},{2,3},{3,2},{4,5},{5,4},{6,7},{7,6},{8,9},{9,8},{10,11... | collective-permute-start | bytes 884744 | tf_op jit(solution)/shard_map/ppermute | solution.py:280
  84.0 4.9 %collective-permute-start.4 = (f32[1,16,1152]{2,1,0:T(8,128)S(1)}, f32[1,16,1152]{2,1,0:T(8,128)S(1)}, u32[]{:S(2)}, u32[]{:S(2)}) collective-permute-start(f32[1,16,1152]{2,1,0:T(8,128)S(1)} %get-tuple-element.14), channel_id=1, source_target_pairs={{0,8},{1,9},{2,10},{3,11},{4,12},{5,13},{6,14},{7,15},{8,0},{9,1},... | collective-permute-start | bytes 221192 | tf_op jit(solution)/shard_map/ppermute | solution.py:280
  84.5 6.2 %collective-permute-start.6 = (f32[1,16,1152]{2,1,0:T(8,128)S(1)}, f32[1,16,1152]{2,1,0:T(8,128)S(1)}, u32[]{:S(2)}, u32[]{:S(2)}) collective-permute-start(f32[1,16,1152]{2,1,0:T(8,128)S(1)} %get-tuple-element.15), channel_id=1, source_target_pairs={{0,24},{1,25},{2,26},{3,27},{4,28},{5,29},{6,30},{7,31},{8,16},{9,... | collective-permute-start | bytes 221192 | tf_op jit(solution)/shard_map/ppermute | solution.py:280
  85.6 7.4 %collective-permute-start.5 = (f32[1,16,1152]{2,1,0:T(8,128)S(1)}, f32[1,16,1152]{2,1,0:T(8,128)S(1)}, u32[]{:S(2)}, u32[]{:S(2)}) collective-permute-start(f32[1,16,1152]{2,1,0:T(8,128)S(1)} %get-tuple-element.16), channel_id=1, source_target_pairs={{0,16},{1,17},{2,18},{3,19},{4,20},{5,21},{6,22},{7,23},{8,24},{9,... | collective-permute-start | bytes 221192 | tf_op jit(solution)/shard_map/ppermute | solution.py:280
  93.0 6.2 %collective-permute-start.9 = (f32[1,16,1152]{2,1,0:T(8,128)S(1)}, f32[1,16,1152]{2,1,0:T(8,128)S(1)}, u32[]{:S(2)}, u32[]{:S(2)}) collective-permute-start(f32[1,16,1152]{2,1,0:T(8,128)S(1)} %get-tuple-element.10), channel_id=1, source_target_pairs={{0,24},{1,25},{2,26},{3,27},{4,28},{5,29},{6,30},{7,31},{8,16},{9,... | collective-permute-start | bytes 221192 | tf_op jit(solution)/shard_map/ppermute | solution.py:280
  95.1 5.6 %collective-permute-start.8 = (f32[1,16,1152]{2,1,0:T(8,128)S(1)}, f32[1,16,1152]{2,1,0:T(8,128)S(1)}, u32[]{:S(2)}, u32[]{:S(2)}) collective-permute-start(f32[1,16,1152]{2,1,0:T(8,128)S(1)} %get-tuple-element.10), channel_id=1, source_target_pairs={{0,16},{1,17},{2,18},{3,19},{4,20},{5,21},{6,22},{7,23},{8,24},{9,... | collective-permute-start | bytes 221192 | tf_op jit(solution)/shard_map/ppermute | solution.py:280
  95.1 5.6 %collective-permute-start.7 = (f32[1,16,1152]{2,1,0:T(8,128)S(1)}, f32[1,16,1152]{2,1,0:T(8,128)S(1)}, u32[]{:S(2)}, u32[]{:S(2)}) collective-permute-start(f32[1,16,1152]{2,1,0:T(8,128)S(1)} %get-tuple-element.10), channel_id=1, source_target_pairs={{0,8},{1,9},{2,10},{3,11},{4,12},{5,13},{6,14},{7,15},{8,0},{9,1},... | collective-permute-start | bytes 221192 | tf_op jit(solution)/shard_map/ppermute | solution.py:280
  100.8 13.0 %collective-permute-start.12 = (f32[4,16,1152]{2,1,0:T(8,128)S(1)}, f32[4,16,1152]{2,1,0:T(8,128)S(1)}, u32[]{:S(2)}, u32[]{:S(2)}) collective-permute-start(f32[4,16,1152]{2,1,0:T(8,128)S(1)} %pad_maximum_fusion), channel_id=1, source_target_pairs={{0,5},{1,4},{2,7},{3,6},{4,1},{5,0},{6,3},{7,2},{8,13},{9,12},{10,... | collective-permute-start | bytes 884744 | tf_op jit(solution)/shard_map/ppermute | solution.py:280
  102.7 11.0 %collective-permute-start.11 = (f32[4,16,1152]{2,1,0:T(8,128)S(1)}, f32[4,16,1152]{2,1,0:T(8,128)S(1)}, u32[]{:S(2)}, u32[]{:S(2)}) collective-permute-start(f32[4,16,1152]{2,1,0:T(8,128)S(1)} %pad_maximum_fusion), channel_id=1, source_target_pairs={{0,1},{1,0},{2,3},{3,2},{4,5},{5,4},{6,7},{7,6},{8,9},{9,8},{10,11... | collective-permute-start | bytes 884744 | tf_op jit(solution)/shard_map/ppermute | solution.py:280
  104.5 9.2 %collective-permute-start.10 = (f32[4,16,1152]{2,1,0:T(8,128)S(1)}, f32[4,16,1152]{2,1,0:T(8,128)S(1)}, u32[]{:S(2)}, u32[]{:S(2)}) collective-permute-start(f32[4,16,1152]{2,1,0:T(8,128)S(1)} %pad_maximum_fusion), channel_id=1, source_target_pairs={{0,4},{1,5},{2,6},{3,7},{4,0},{5,1},{6,2},{7,3},{8,12},{9,13},{10,... | collective-permute-start | bytes 884744 | tf_op jit(solution)/shard_map/ppermute | solution.py:280
  113.8 2.9 %collective-permute-start.13 = (f32[16,16,1152]{2,1,0:T(8,128)S(1)}, f32[16,16,1152]{2,1,0:T(8,128)S(1)}, u32[]{:S(2)}, u32[]{:S(2)}) collective-permute-start(f32[16,16,1152]{2,1,0:T(8,128)S(1)} %constant_dynamic-update-slice_fusion.own_ref), channel_id=1, source_target_pairs={{0,2},{1,3},{2,0},{3,1},{4,6},{5,7},{6,4},{7,5},{8,10},{9,11},{10,... | collective-permute-start | bytes 3538952 | tf_op jit(solution)/shard_map/ppermute | solution.py:280

commit v2 on v1

--- a/solution.py
+++ b/solution.py
@@ -80,10 +80,27 @@
     )
 
 
-def mm(a,b,dims=(((1,),(0,)),((),()))):
-    return lax.dot_general(a,b,dims,precision=HI,preferred_element_type=f32)
-TA=(((0,),(0,)),((),()))
-TB=(((1,),(1,)),((),()))
+TA = (((0,), (0,)), ((), ()))
+LEFT = (0, 0, 1, 0, 2, 1)
+RIGHT = (0, 1, 0, 2, 0, 1)
+
+
+def split(x):
+    hi = x.astype(jnp.bfloat16)
+    rest = x - hi.astype(f32)
+    mid = rest.astype(jnp.bfloat16)
+    return hi, mid, (rest - mid.astype(f32)).astype(jnp.bfloat16)
+
+
+def mm6(a, b, ca, cb):
+    lhs = jnp.concatenate([a[i] for i in LEFT], axis=ca)
+    rhs = jnp.concatenate([b[i] for i in RIGHT], axis=cb)
+    return lax.dot_general(lhs, rhs, (((ca,), (cb,)), ((), ())), preferred_element_type=f32)
+
+
+def mm(a, b, dims=(((1,), (0,)), ((), ()))):
+    return mm6(split(a), split(b), dims[0][0][0], dims[0][1][0])
+
 
 def elim(X, sbase, ibase, n, zero=None):
     G=n//8
@@ -206,10 +223,10 @@
     lax.fori_loop(0, half, put, 0)
 
 
-def factor_kernel(n, pos_ref, own_ref, recv_ref, out_ref, fold, u_ref, strip, zref, turn):
+def factor_kernel(n, pos_ref, own_ref, recv_ref, out_ref, fold, u_ref, strip, zref, turn, w_ref, uh, um, ul):
     B = TILE
     nb = n // B
-    CW = 2 * B
+    parts = (uh, um, ul)
     half = own_ref.shape[0]
     h = own_ref.shape[1]
     me = pos_ref[0]
@@ -222,44 +239,33 @@
     lax.fori_loop(0, half, get, 0)
     zref[...] = jnp.zeros((8, 128), f32)
 
+    def update(k):
+        right = slice(k * B, n)
+        panel, off = (k, 0) if k < nb // 2 else (nb - 1 - k, k + 1)
+        rows = fold[panel * B : (panel + 1) * B, off * B : (off + nb - k) * B]
+        if k:
+            cols = slice(k * B, (k + 1) * B)
+            rows = rows - mm6([u[: k * B, cols] for u in parts], [u[: k * B, right] for u in parts], 0, 0)
+        strip[:, right] = rows
+
+    def solve(k):
+        if k == nb - 1:
+            return
+        right = slice((k + 1) * B, n)
+        done = mm6(split(w_ref[...]), split(strip[:, right]), 1, 0)
+        u_ref[k * B : (k + 1) * B, right] = done
+        for u, v in zip(parts, split(done)):
+            u[k * B : (k + 1) * B, right] = v
+
     def body(k, _):
+        for kk in range(nb):
+            pl.when(k == kk)(functools.partial(update, kk))
         kc = pl.multiple_of(k * B, B)
-        low = k < nb // 2
-        panel = jnp.where(low, k, nb - 1 - k)
-        off = jnp.where(low, -k, 1)
-
-        def load(c, _):
-            src = pl.multiple_of((c + off) * B, B)
-            strip[:, pl.ds(pl.multiple_of(c * B, B), B)] = fold[
-                pl.ds(pl.multiple_of(panel * B, B), B), pl.ds(src, B)
-            ]
-            return 0
-
-        lax.fori_loop(k, nb, load, 0)
-        c0 = kc // CW
-        nc = n // CW
-
-        def chunk(c, _):
-            cc = pl.multiple_of(c * CW, CW)
-
-            def kk(j, acc):
-                jj = pl.multiple_of(j * B, B)
-                return acc + mm(u_ref[pl.ds(jj, B), pl.ds(kc, B)], u_ref[pl.ds(jj, B), pl.ds(cc, CW)], TA)
-
-            acc = lax.fori_loop(0, k, kk, jnp.zeros((B, CW), f32))
-            strip[:, pl.ds(cc, CW)] = strip[:, pl.ds(cc, CW)] - acc
-            return 0
-
-        lax.fori_loop(c0, nc, chunk, 0)
         U, W = factor128(strip[:, pl.ds(kc, B)], zref[...])
-
-        def pan(c, _):
-            cc = pl.multiple_of(c * CW, CW)
-            u_ref[pl.ds(kc, B), pl.ds(cc, CW)] = mm(W, strip[:, pl.ds(cc, CW)])
-            return 0
-
-        lax.fori_loop(c0, nc, pan, 0)
+        w_ref[...] = W
         u_ref[pl.ds(kc, B), pl.ds(kc, B)] = U
+        for kk in range(nb):
+            pl.when(k == kk)(functools.partial(solve, kk))
         return 0
 
     lax.fori_loop(0, nb, body, 0)
@@ -363,7 +369,9 @@
             pltpu.VMEM((TILE, n), f32),
             pltpu.VMEM((8, 128), f32),
             pltpu.VMEM((TILE, TILE), f32),
-        ],
+            pltpu.VMEM((TILE, TILE), f32),
+        ]
+        + [pltpu.VMEM((n, n), jnp.bfloat16)] * 3,
         compiler_params=pltpu.CompilerParams(vmem_limit_bytes=40 << 20),
         name="factor",
     )(jnp.stack([place, row_i, grp_i]), total, other)

time: 169 us -> 153 us (0.905)
  Pallas kernels: 53.5 us -> 37.4 us
    pallas_call x1, Pallas kernels: 51.7 us -> 35.6 us  [local_fast(): pl.pallas_call(functools.partial(factor_kernel, n), out_shape=jax.ShapeDt...]
  transfers between devices with their start and end apart: 15 -> 15, of which waited for: 12 -> 12; matrix products, arithmetic and copies ran while one was open for 1% -> 2% of each run, Pallas kernels for 0% -> 0%
where the time goes in v2:
time: 153 us; the launch traced here: 152 us
  waiting for transfers between devices  84.2 us (55%)
  Pallas kernels  37.4 us (24%)
  starting transfers between devices  22.8 us (15%)
  matrix products  4.15 us (3%)
  other arithmetic  3.32 us (2%)
    all_to_all x1, waiting for transfers between devices, local_fast(): lax.all_to_all(local_mix, AXES, split_axis=0, concat_axis=0, tiled=True)  46.3 us
    ppermute x14, waiting for transfers between devices, xor_send(): return lax.ppermute(value, AXES, [(d, d ^ mask) for d in range(n_dev)])  37.9 us
    pallas_call x1, Pallas kernels, local_fast(): pl.pallas_call(functools.partial(factor_kernel, n), out_shape=jax.ShapeDt...  35.6 us
    ppermute x14, starting transfers between devices, xor_send(): return lax.ppermute(value, AXES, [(d, d ^ mask) for d in range(n_dev)])  15.4 us
    all_to_all x1, starting transfers between devices, local_fast(): lax.all_to_all(local_mix, AXES, split_axis=0, concat_axis=0, tiled=True)  7.32 us
    dot_general x1, matrix products, local_fast(): jnp.dot(hadamard(rows_dev, jnp.bfloat16), flipped, preferred_element_type...  4.15 us
  transfers between devices with their start and end apart: 15, of which 12 were waited for; matrix products, arithmetic and copies ran while one was open for 2% of the time, Pallas kernels for 0%

profile of v2, /device:TPU:0, one launch (start us, length us, event | category | flops | bytes accessed | tf_op | source)
XLA Modules:
  0.0 152.3 jit_solution(813774703858483448)
XLA Ops:
  0.7 4.2 %fusion = f32[512,1024]{1,0:T(8,128)} fusion(bf16[512,1024]{1,0:T(8,128)(2,1)} %param.3, bf16[512]{0:T(512)(128)(2,1)S(1)} %subtract_convert_fusion.2), kind=kOutput, calls=%fused_computation.1 | convolution fusion | flops 545259520 | bytes 3146752 | tf_op jit(solution)/shard_map/dot_general | solution.py:302
  4.8 7.3 %all-to-all-start = ((f32[32,16,1024]{2,1,0:T(8,128)}), f32[32,16,1024]{2,1,0:T(8,128)S(1)}, u32[]{:S(2)}, u32[]{:S(2)}) async-start(f32[32,16,1024]{2,1,0:T(8,128)} %bitcast.4), calls=%async_computation | async-start | bytes 4194304 | tf_op jit(solution)/shard_map/all_to_all | solution.py:303
  12.3 2.3 %compare_reduce_fusion = pred[512]{0:T(512)(128)(4,1)S(1)} fusion(s32[8192]{0:T(1024)S(1)} %copy-done, s32[512]{0:T(512)S(1)} %fusion.24), kind=kLoop, calls=%fused_computation | loop fusion | flops 8388096 | bytes 35328 | tf_op jit(solution)/shard_map/reduce_or | solution.py:308
  14.5 46.3 %all-to-all-done.x_ref = f32[32,16,1024]{2,1,0:T(8,128)S(1)} async-done(((f32[32,16,1024]{2,1,0:T(8,128)}), f32[32,16,1024]{2,1,0:T(8,128)S(1)}, u32[]{:S(2)}, u32[]{:S(2)}) %all-to-all-start) | async-done | bytes 2097184 | tf_op jit(solution)/shard_map/all_to_all | solution.py:303
  61.0 1.8 %sketch_gram.1 = (f32[16,16,1152]{2,1,0:T(8,128)S(1)}, f32[16,16,1152]{2,1,0:T(8,128)S(1)}) custom-call(s32[1]{0:T(128)} %bitcast.me_ref, f32[32,16,1024]{2,1,0:T(8,128)S(1)} %all-to-all-done.x_ref, f32[512,128]{1,0:T(8,128)S(1)} %broadcast_in_dim.20.m_ref), custom_call_target="tpu_custom_call" | custom-call | tf_op jit(solution)/shard_map/sketch_gram/pallas_call | solution.py:331
  62.9 2.8 %collective-permute-done = f32[16,16,1152]{2,1,0:T(8,128)S(1)} collective-permute-done((f32[16,16,1152]{2,1,0:T(8,128)S(1)}, f32[16,16,1152]{2,1,0:T(8,128)S(1)}, u32[]{:S(2)}, u32[]{:S(2)}) %collective-permute-start) | collective-permute-done | bytes 1179680 | tf_op jit(solution)/shard_map/ppermute | solution.py:286
  65.9 1.5 %collective-permute-start.1 = (f32[4,16,1152]{2,1,0:T(8,128)S(1)}, f32[4,16,1152]{2,1,0:T(8,128)S(1)}, u32[]{:S(2)}, u32[]{:S(2)}) collective-permute-start(f32[4,16,1152]{2,1,0:T(8,128)S(1)} %get-tuple-element.11), channel_id=1, source_target_pairs={{0,4},{1,5},{2,6},{3,7},{4,0},{5,1},{6,2},{7,3},{8,12},{9,13},{10,... | collective-permute-start | bytes 884744 | tf_op jit(solution)/shard_map/ppermute | solution.py:286
  67.5 1.6 %collective-permute-start.3 = (f32[4,16,1152]{2,1,0:T(8,128)S(1)}, f32[4,16,1152]{2,1,0:T(8,128)S(1)}, u32[]{:S(2)}, u32[]{:S(2)}) collective-permute-start(f32[4,16,1152]{2,1,0:T(8,128)S(1)} %get-tuple-element.12), channel_id=1, source_target_pairs={{0,5},{1,4},{2,7},{3,6},{4,1},{5,0},{6,3},{7,2},{8,13},{9,12},{10,... | collective-permute-start | bytes 884744 | tf_op jit(solution)/shard_map/ppermute | solution.py:286
  69.5 6.4 %collective-permute-done.1 = f32[4,16,1152]{2,1,0:T(8,128)S(1)} collective-permute-done((f32[4,16,1152]{2,1,0:T(8,128)S(1)}, f32[4,16,1152]{2,1,0:T(8,128)S(1)}, u32[]{:S(2)}, u32[]{:S(2)}) %collective-permute-start.1) | collective-permute-done | bytes 294944 | tf_op jit(solution)/shard_map/ppermute | solution.py:286
  75.9 6.7 %collective-permute-done.3 = f32[4,16,1152]{2,1,0:T(8,128)S(1)} collective-permute-done((f32[4,16,1152]{2,1,0:T(8,128)S(1)}, f32[4,16,1152]{2,1,0:T(8,128)S(1)}, u32[]{:S(2)}, u32[]{:S(2)}) %collective-permute-start.3) | collective-permute-done | bytes 294944 | tf_op jit(solution)/shard_map/ppermute | solution.py:286
  82.5 1.4 collective-permute-done.2
  85.6 2.0 %collective-permute-start.5 = (f32[1,16,1152]{2,1,0:T(8,128)S(1)}, f32[1,16,1152]{2,1,0:T(8,128)S(1)}, u32[]{:S(2)}, u32[]{:S(2)}) collective-permute-start(f32[1,16,1152]{2,1,0:T(8,128)S(1)} %get-tuple-element.16), channel_id=1, source_target_pairs={{0,16},{1,17},{2,18},{3,19},{4,20},{5,21},{6,22},{7,23},{8,24},{9,... | collective-permute-start | bytes 221192 | tf_op jit(solution)/shard_map/ppermute | solution.py:286
  87.5 1.4 collective-permute-done.4
  88.9 1.8 %collective-permute-done.6 = f32[1,16,1152]{2,1,0:T(8,128)S(1)} collective-permute-done((f32[1,16,1152]{2,1,0:T(8,128)S(1)}, f32[1,16,1152]{2,1,0:T(8,128)S(1)}, u32[]{:S(2)}, u32[]{:S(2)}) %collective-permute-start.6) | collective-permute-done | bytes 73760 | tf_op jit(solution)/shard_map/ppermute | solution.py:286
  90.7 2.2 %collective-permute-done.5 = f32[1,16,1152]{2,1,0:T(8,128)S(1)} collective-permute-done((f32[1,16,1152]{2,1,0:T(8,128)S(1)}, f32[1,16,1152]{2,1,0:T(8,128)S(1)}, u32[]{:S(2)}, u32[]{:S(2)}) %collective-permute-start.5) | collective-permute-done | bytes 73760 | tf_op jit(solution)/shard_map/ppermute | solution.py:286
  93.0 2.2 %collective-permute-start.9 = (f32[1,16,1152]{2,1,0:T(8,128)S(1)}, f32[1,16,1152]{2,1,0:T(8,128)S(1)}, u32[]{:S(2)}, u32[]{:S(2)}) collective-permute-start(f32[1,16,1152]{2,1,0:T(8,128)S(1)} %get-tuple-element.10), channel_id=1, source_target_pairs={{0,24},{1,25},{2,26},{3,27},{4,28},{5,29},{6,30},{7,31},{8,16},{9,... | collective-permute-start | bytes 221192 | tf_op jit(solution)/shard_map/ppermute | solution.py:286
  95.1 2.3 %collective-permute-start.7 = (f32[1,16,1152]{2,1,0:T(8,128)S(1)}, f32[1,16,1152]{2,1,0:T(8,128)S(1)}, u32[]{:S(2)}, u32[]{:S(2)}) collective-permute-start(f32[1,16,1152]{2,1,0:T(8,128)S(1)} %get-tuple-element.10), channel_id=1, source_target_pairs={{0,8},{1,9},{2,10},{3,11},{4,12},{5,13},{6,14},{7,15},{8,0},{9,1},... | collective-permute-start | bytes 221192 | tf_op jit(solution)/shard_map/ppermute | solution.py:286
  97.4 1.8 %collective-permute-done.9 = f32[1,16,1152]{2,1,0:T(8,128)S(1)} collective-permute-done((f32[1,16,1152]{2,1,0:T(8,128)S(1)}, f32[1,16,1152]{2,1,0:T(8,128)S(1)}, u32[]{:S(2)}, u32[]{:S(2)}) %collective-permute-start.9) | collective-permute-done | bytes 73760 | tf_op jit(solution)/shard_map/ppermute | solution.py:286
  99.2 1.6 %collective-permute-done.8 = f32[1,16,1152]{2,1,0:T(8,128)S(1)} collective-permute-done((f32[1,16,1152]{2,1,0:T(8,128)S(1)}, f32[1,16,1152]{2,1,0:T(8,128)S(1)}, u32[]{:S(2)}, u32[]{:S(2)}) %collective-permute-start.8) | collective-permute-done | bytes 73760 | tf_op jit(solution)/shard_map/ppermute | solution.py:286
  100.8 1.9 %collective-permute-start.12 = (f32[4,16,1152]{2,1,0:T(8,128)S(1)}, f32[4,16,1152]{2,1,0:T(8,128)S(1)}, u32[]{:S(2)}, u32[]{:S(2)}) collective-permute-start(f32[4,16,1152]{2,1,0:T(8,128)S(1)} %pad_maximum_fusion), channel_id=1, source_target_pairs={{0,5},{1,4},{2,7},{3,6},{4,1},{5,0},{6,3},{7,2},{8,13},{9,12},{10,... | collective-permute-start | bytes 884744 | tf_op jit(solution)/shard_map/ppermute | solution.py:286
  102.7 1.8 %collective-permute-start.11 = (f32[4,16,1152]{2,1,0:T(8,128)S(1)}, f32[4,16,1152]{2,1,0:T(8,128)S(1)}, u32[]{:S(2)}, u32[]{:S(2)}) collective-permute-start(f32[4,16,1152]{2,1,0:T(8,128)S(1)} %pad_maximum_fusion), channel_id=1, source_target_pairs={{0,1},{1,0},{2,3},{3,2},{4,5},{5,4},{6,7},{7,6},{8,9},{9,8},{10,11... | collective-permute-start | bytes 884744 | tf_op jit(solution)/shard_map/ppermute | solution.py:286
  104.6 9.1 %collective-permute-done.10 = f32[4,16,1152]{2,1,0:T(8,128)S(1)} collective-permute-done((f32[4,16,1152]{2,1,0:T(8,128)S(1)}, f32[4,16,1152]{2,1,0:T(8,128)S(1)}, u32[]{:S(2)}, u32[]{:S(2)}) %collective-permute-start.10) | collective-permute-done | bytes 294944 | tf_op jit(solution)/shard_map/ppermute | solution.py:286
  113.9 2.8 %collective-permute-done.13.recv_ref = f32[16,16,1152]{2,1,0:T(8,128)S(1)} collective-permute-done((f32[16,16,1152]{2,1,0:T(8,128)S(1)}, f32[16,16,1152]{2,1,0:T(8,128)S(1)}, u32[]{:S(2)}, u32[]{:S(2)}) %collective-permute-start.13) | collective-permute-done | bytes 1179680 | tf_op jit(solution)/shard_map/ppermute | solution.py:286
  116.7 35.6 %factor.1 = f32[64,512]{1,0:T(8,128)} custom-call(s32[3]{0:T(128)S(1)} %pad_add_fusion.pos_ref, f32[16,16,1152]{2,1,0:T(8,128)S(1)} %constant_dynamic-update-slice_fusion.own_ref, f32[16,16,1152]{2,1,0:T(8,128)S(1)} %collective-permute-done.13.recv_ref), custom_call_target="tpu_custom_call" | custom-call | tf_op jit(solution)/shard_map/factor/pallas_call | solution.py:361
  (29 shorter events, 3.4 us)
Async XLA Ops:
  4.8 7.4 %copy-start = (s32[8192]{0:T(1024)S(1)}, s32[8192]{0:T(1024)}, u32[]{:S(2)}) copy-start(s32[8192]{0:T(1024)} %param.5) | copy-start | bytes 98308
  4.8 56.0 %all-to-all-start = ((f32[32,16,1024]{2,1,0:T(8,128)}), f32[32,16,1024]{2,1,0:T(8,128)S(1)}, u32[]{:S(2)}, u32[]{:S(2)}) async-start(f32[32,16,1024]{2,1,0:T(8,128)} %bitcast.4), calls=%async_computation | async-start | bytes 4194304 | tf_op jit(solution)/shard_map/all_to_all | solution.py:303
  62.8 2.9 %collective-permute-start = (f32[16,16,1152]{2,1,0:T(8,128)S(1)}, f32[16,16,1152]{2,1,0:T(8,128)S(1)}, u32[]{:S(2)}, u32[]{:S(2)}) collective-permute-start(f32[16,16,1152]{2,1,0:T(8,128)S(1)} %get-tuple-element.8), channel_id=1, source_target_pairs={{0,2},{1,3},{2,0},{3,1},{4,6},{5,7},{6,4},{7,5},{8,10},{9,11},{10,... | collective-permute-start | bytes 3538952 | tf_op jit(solution)/shard_map/ppermute | solution.py:286
  65.9 9.9 %collective-permute-start.1 = (f32[4,16,1152]{2,1,0:T(8,128)S(1)}, f32[4,16,1152]{2,1,0:T(8,128)S(1)}, u32[]{:S(2)}, u32[]{:S(2)}) collective-permute-start(f32[4,16,1152]{2,1,0:T(8,128)S(1)} %get-tuple-element.11), channel_id=1, source_target_pairs={{0,4},{1,5},{2,6},{3,7},{4,0},{5,1},{6,2},{7,3},{8,12},{9,13},{10,... | collective-permute-start | bytes 884744 | tf_op jit(solution)/shard_map/ppermute | solution.py:286
  67.5 15.1 %collective-permute-start.3 = (f32[4,16,1152]{2,1,0:T(8,128)S(1)}, f32[4,16,1152]{2,1,0:T(8,128)S(1)}, u32[]{:S(2)}, u32[]{:S(2)}) collective-permute-start(f32[4,16,1152]{2,1,0:T(8,128)S(1)} %get-tuple-element.12), channel_id=1, source_target_pairs={{0,5},{1,4},{2,7},{3,6},{4,1},{5,0},{6,3},{7,2},{8,13},{9,12},{10,... | collective-permute-start | bytes 884744 | tf_op jit(solution)/shard_map/ppermute | solution.py:286
  69.1 14.8 %collective-permute-start.2 = (f32[4,16,1152]{2,1,0:T(8,128)S(1)}, f32[4,16,1152]{2,1,0:T(8,128)S(1)}, u32[]{:S(2)}, u32[]{:S(2)}) collective-permute-start(f32[4,16,1152]{2,1,0:T(8,128)S(1)} %get-tuple-element.13), channel_id=1, source_target_pairs={{0,1},{1,0},{2,3},{3,2},{4,5},{5,4},{6,7},{7,6},{8,9},{9,8},{10,11... | collective-permute-start | bytes 884744 | tf_op jit(solution)/shard_map/ppermute | solution.py:286
  84.0 4.9 %collective-permute-start.4 = (f32[1,16,1152]{2,1,0:T(8,128)S(1)}, f32[1,16,1152]{2,1,0:T(8,128)S(1)}, u32[]{:S(2)}, u32[]{:S(2)}) collective-permute-start(f32[1,16,1152]{2,1,0:T(8,128)S(1)} %get-tuple-element.14), channel_id=1, source_target_pairs={{0,8},{1,9},{2,10},{3,11},{4,12},{5,13},{6,14},{7,15},{8,0},{9,1},... | collective-permute-start | bytes 221192 | tf_op jit(solution)/shard_map/ppermute | solution.py:286
  84.5 6.2 %collective-permute-start.6 = (f32[1,16,1152]{2,1,0:T(8,128)S(1)}, f32[1,16,1152]{2,1,0:T(8,128)S(1)}, u32[]{:S(2)}, u32[]{:S(2)}) collective-permute-start(f32[1,16,1152]{2,1,0:T(8,128)S(1)} %get-tuple-element.15), channel_id=1, source_target_pairs={{0,24},{1,25},{2,26},{3,27},{4,28},{5,29},{6,30},{7,31},{8,16},{9,... | collective-permute-start | bytes 221192 | tf_op jit(solution)/shard_map/ppermute | solution.py:286
  85.6 7.4 %collective-permute-start.5 = (f32[1,16,1152]{2,1,0:T(8,128)S(1)}, f32[1,16,1152]{2,1,0:T(8,128)S(1)}, u32[]{:S(2)}, u32[]{:S(2)}) collective-permute-start(f32[1,16,1152]{2,1,0:T(8,128)S(1)} %get-tuple-element.16), channel_id=1, source_target_pairs={{0,16},{1,17},{2,18},{3,19},{4,20},{5,21},{6,22},{7,23},{8,24},{9,... | collective-permute-start | bytes 221192 | tf_op jit(solution)/shard_map/ppermute | solution.py:286
  93.0 6.2 %collective-permute-start.9 = (f32[1,16,1152]{2,1,0:T(8,128)S(1)}, f32[1,16,1152]{2,1,0:T(8,128)S(1)}, u32[]{:S(2)}, u32[]{:S(2)}) collective-permute-start(f32[1,16,1152]{2,1,0:T(8,128)S(1)} %get-tuple-element.10), channel_id=1, source_target_pairs={{0,24},{1,25},{2,26},{3,27},{4,28},{5,29},{6,30},{7,31},{8,16},{9,... | collective-permute-start | bytes 221192 | tf_op jit(solution)/shard_map/ppermute | solution.py:286
  95.1 5.6 %collective-permute-start.8 = (f32[1,16,1152]{2,1,0:T(8,128)S(1)}, f32[1,16,1152]{2,1,0:T(8,128)S(1)}, u32[]{:S(2)}, u32[]{:S(2)}) collective-permute-start(f32[1,16,1152]{2,1,0:T(8,128)S(1)} %get-tuple-element.10), channel_id=1, source_target_pairs={{0,16},{1,17},{2,18},{3,19},{4,20},{5,21},{6,22},{7,23},{8,24},{9,... | collective-permute-start | bytes 221192 | tf_op jit(solution)/shard_map/ppermute | solution.py:286
  95.1 5.6 %collective-permute-start.7 = (f32[1,16,1152]{2,1,0:T(8,128)S(1)}, f32[1,16,1152]{2,1,0:T(8,128)S(1)}, u32[]{:S(2)}, u32[]{:S(2)}) collective-permute-start(f32[1,16,1152]{2,1,0:T(8,128)S(1)} %get-tuple-element.10), channel_id=1, source_target_pairs={{0,8},{1,9},{2,10},{3,11},{4,12},{5,13},{6,14},{7,15},{8,0},{9,1},... | collective-permute-start | bytes 221192 | tf_op jit(solution)/shard_map/ppermute | solution.py:286
  100.8 13.0 %collective-permute-start.12 = (f32[4,16,1152]{2,1,0:T(8,128)S(1)}, f32[4,16,1152]{2,1,0:T(8,128)S(1)}, u32[]{:S(2)}, u32[]{:S(2)}) collective-permute-start(f32[4,16,1152]{2,1,0:T(8,128)S(1)} %pad_maximum_fusion), channel_id=1, source_target_pairs={{0,5},{1,4},{2,7},{3,6},{4,1},{5,0},{6,3},{7,2},{8,13},{9,12},{10,... | collective-permute-start | bytes 884744 | tf_op jit(solution)/shard_map/ppermute | solution.py:286
  102.7 11.0 %collective-permute-start.11 = (f32[4,16,1152]{2,1,0:T(8,128)S(1)}, f32[4,16,1152]{2,1,0:T(8,128)S(1)}, u32[]{:S(2)}, u32[]{:S(2)}) collective-permute-start(f32[4,16,1152]{2,1,0:T(8,128)S(1)} %pad_maximum_fusion), channel_id=1, source_target_pairs={{0,1},{1,0},{2,3},{3,2},{4,5},{5,4},{6,7},{7,6},{8,9},{9,8},{10,11... | collective-permute-start | bytes 884744 | tf_op jit(solution)/shard_map/ppermute | solution.py:286
  104.5 9.2 %collective-permute-start.10 = (f32[4,16,1152]{2,1,0:T(8,128)S(1)}, f32[4,16,1152]{2,1,0:T(8,128)S(1)}, u32[]{:S(2)}, u32[]{:S(2)}) collective-permute-start(f32[4,16,1152]{2,1,0:T(8,128)S(1)} %pad_maximum_fusion), channel_id=1, source_target_pairs={{0,4},{1,5},{2,6},{3,7},{4,0},{5,1},{6,2},{7,3},{8,12},{9,13},{10,... | collective-permute-start | bytes 884744 | tf_op jit(solution)/shard_map/ppermute | solution.py:286
  113.8 2.9 %collective-permute-start.13 = (f32[16,16,1152]{2,1,0:T(8,128)S(1)}, f32[16,16,1152]{2,1,0:T(8,128)S(1)}, u32[]{:S(2)}, u32[]{:S(2)}) collective-permute-start(f32[16,16,1152]{2,1,0:T(8,128)S(1)} %constant_dynamic-update-slice_fusion.own_ref), channel_id=1, source_target_pairs={{0,2},{1,3},{2,0},{3,1},{4,6},{5,7},{6,4},{7,5},{8,10},{9,11},{10,... | collective-permute-start | bytes 3538952 | tf_op jit(solution)/shard_map/ppermute | solution.py:286

commit v3 on v2

--- a/solution.py
+++ b/solution.py
@@ -11,7 +11,6 @@
 AXES = ("row", "grp")
 TILE = 128
 f32 = jnp.float32
-HI = lax.Precision.HIGHEST
 
 
 def hadamard(table_size, dtype):
@@ -98,83 +97,83 @@
     return lax.dot_general(lhs, rhs, (((ca,), (cb,)), ((), ())), preferred_element_type=f32)
 
 
-def mm(a, b, dims=(((1,), (0,)), ((), ()))):
-    return mm6(split(a), split(b), dims[0][0][0], dims[0][1][0])
-
-
-def elim(X, sbase, ibase, n, zero=None):
-    G=n//8
-    xs=[X[8*g:8*g+8,:] for g in range(G)]
-    rid=lax.broadcasted_iota(jnp.int32,(8,128),0)
-    full=lambda v: jnp.broadcast_to(v,(8,128))
-    out=[]
+def eliminate(X, first, zero):
+    G = X.shape[0] // 8
+    xs = [X[8 * g : 8 * g + 8, :] for g in range(G)]
+    rid = lax.broadcasted_iota(jnp.int32, (8, TILE), 0)
+
+    def full(v):
+        return jnp.broadcast_to(v, (8, TILE))
+
+    def col(h, at):
+        return full(xs[h][:, first + at : first + at + 1])
+
+    out = []
+    D = [col(0, m) + zero for m in range(8)]
     for g in range(G):
-        C=[[None]*G for _ in range(8)]
-        for m in range(8):
-            for h in range(g,G):
-                l=sbase+8*g+m
-                C[m][h]=full(xs[h][:,l:l+1])
-        for m in range(8): C[m][g]=C[m][g]+zero
-        o=jnp.zeros((8,128),f32)
-        for j in range(0,8,2):
-            a=full(C[j][g][j:j+1,:]); b=full(C[j][g][j+1:j+2,:]); c=full(C[j+1][g][j+1:j+2,:])
-            r0=full(xs[g][j:j+1,:]); r1=full(xs[g][j+1:j+2,:])
-            det=a*c-b*b
-            inv=1.0/det
-            ws=[]
-            for m in range(j+2,8):
-                q0=full(C[m][g][j:j+1,:]); q1=full(C[m][g][j+1:j+2,:])
-                if j==0:
-                    q0=q0; q1=q1
-                ws.append((m,(c*q0-b*q1)*inv,(a*q1-b*q0)*inv))
-            t1=a*r1-b*r0
-            u0=(c*r0-b*r1)*inv; u1=t1*inv
-            for m,w0,w1 in ws:
-                for h in range(g,G):
-                    C[m][h]=C[m][h]-C[j][h]*w0-C[j+1][h]*w1
-            for h in range(g,G):
-                if h>g or j<6:
-                    xs[h]=xs[h]-C[j][h]*u0-C[j+1][h]*u1
-            l0=r0*lax.rsqrt(a); l1=t1*lax.rsqrt(a*det)
-            o=jnp.where(rid==j,l0,jnp.where(rid==j+1,l1,o))
+        C = D
+        more = g + 1 < G
+        near = [col(g + 1, 8 * g + m) for m in range(8)] if more else None
+        D = [col(g + 1, 8 * g + 8 + m) for m in range(8)] if more else None
+        far = {h: [col(h, 8 * g + m) for m in range(8)] for h in range(g + 2, G)}
+        o = jnp.zeros((8, TILE), f32)
+        for j in range(0, 8, 2):
+            a = full(C[j][j : j + 1, :])
+            b = full(C[j][j + 1 : j + 2, :])
+            c = full(C[j + 1][j + 1 : j + 2, :])
+            det = a * c - b * b
+            inv = 1.0 / det
+            ws = {}
+            for m in range(j + 2, 8):
+                q0 = full(C[m][j : j + 1, :])
+                q1 = full(C[m][j + 1 : j + 2, :])
+                t0 = c * q0 - b * q1
+                t1 = a * q1 - b * q0
+                ws[m] = t0 * inv, t1 * inv
+                C[m] = C[m] - (C[j] * t0 + C[j + 1] * t1) * inv
+            if more:
+                n0 = c * near[j] - b * near[j + 1]
+                n1 = a * near[j + 1] - b * near[j]
+                if j == 6:
+                    for m in range(8):
+                        D[m] = D[m] - (near[j] * full(n0[m : m + 1, :]) + near[j + 1] * full(n1[m : m + 1, :])) * inv
+                else:
+                    v0 = n0 * inv
+                    v1 = n1 * inv
+                    for m in range(8):
+                        D[m] = D[m] - near[j] * full(v0[m : m + 1, :]) - near[j + 1] * full(v1[m : m + 1, :])
+            r0 = full(xs[g][j : j + 1, :])
+            r1 = full(xs[g][j + 1 : j + 2, :])
+            t1 = a * r1 - b * r0
+            u0 = (c * r0 - b * r1) * inv
+            u1 = t1 * inv
+            if j < 6:
+                xs[g] = xs[g] - C[j] * u0 - C[j + 1] * u1
+            if more:
+                xs[g + 1] = xs[g + 1] - near[j] * u0 - near[j + 1] * u1
+                for m, (w0, w1) in ws.items():
+                    near[m] = near[m] - near[j] * w0 - near[j + 1] * w1
+            for h, cols in far.items():
+                xs[h] = xs[h] - cols[j] * u0 - cols[j + 1] * u1
+                for m, (w0, w1) in ws.items():
+                    cols[m] = cols[m] - cols[j] * w0 - cols[j + 1] * w1
+            l0 = r0 * lax.rsqrt(a)
+            l1 = t1 * lax.rsqrt(a * det)
+            o = jnp.where(rid == j, l0, jnp.where(rid == j + 1, l1, o))
         out.append(o)
-    return jnp.concatenate(out,axis=0)
-
-def factor128(D,zero):
-    lane=lax.broadcasted_iota(jnp.int32,(64,128),1)
-    row=lax.broadcasted_iota(jnp.int32,(64,128),0)
-    z=jnp.zeros((64,128),f32)
-    def equil(S,off,ioff):
-        e=lane==row+off
-        dg=jnp.where(e,S,0.0)
-        dc=lax.rsqrt(jnp.sum(dg,axis=1,keepdims=True))
-        dsum=jnp.sum(dg,axis=0,keepdims=True)
-        half=(lane>=off)&(lane<off+64)
-        drow=jnp.where(half[0:1],dsum,1.0)
-        dr=lax.rsqrt(drow)
-        X=jnp.where(half,S*dc*dr,jnp.where(lane==row+ioff,dc,0.0))
-        back=jnp.where(half[0:1],drow*dr,1.0)
-        return X,back
-    Dt=D[:64,:]; Db=D[64:,:]
-    X1,bk1=equil(Dt,0,64)
-    F1=elim(X1,0,64,64,zero)*bk1
-    U1=mm(F1,jnp.concatenate([z,Dt],axis=0))
-    U12=jnp.where(lane>=64,U1,0.0)
-    T=mm(U12,U12,TA)
-    D2=Db-T[64:,:]
-    X2,bk2=equil(D2,64,0)
-    F2=elim(X2,64,0,64,zero)*bk2
-    W1=jnp.where(lane>=64,F1,0.0)
-    Q=mm(U12,F1,TA)
-    V=mm(F2,jnp.concatenate([Q[64:,:],z],axis=0))
-    W1s=pltpu.roll(F1,64,1); Vs=pltpu.roll(V,64,1)
-    lo=lane<64
-    Wtop=jnp.where(lo,W1s,0.0)
-    W2s=pltpu.roll(F2,64,1)
-    Wbot=jnp.where(lo,-Vs,W2s)
-    Utop=jnp.where(lo,jnp.where(lane>=row,F1,0.0),U1)
-    Ubot=jnp.where((~lo)&(lane-64>=row),F2,0.0)
-    return jnp.concatenate([Utop,Ubot],axis=0),jnp.concatenate([Wtop,Wbot],axis=0)
+    return jnp.concatenate(out, axis=0)
+
+
+def scaled(S, off, other):
+    lane = lax.broadcasted_iota(jnp.int32, S.shape, 1)
+    row = lax.broadcasted_iota(jnp.int32, S.shape, 0)
+    diag = jnp.where(lane == row + off, S, 0.0)
+    down = lax.rsqrt(jnp.sum(diag, axis=1, keepdims=True))
+    half = (lane >= off) & (lane < off + S.shape[0])
+    across = jnp.where(half[0:1], jnp.sum(diag, axis=0, keepdims=True), 1.0)
+    root = lax.rsqrt(across)
+    X = jnp.where(half, S * down * root, jnp.where(lane == row + other, down, 0.0))
+    return X, jnp.where(half[0:1], across * root, 1.0)
 
 
 def sketch_gram_kernel(n_dev, me_ref, x_ref, m_ref, keep_ref, send_ref, s_ref, fold):
@@ -223,8 +222,9 @@
     lax.fori_loop(0, half, put, 0)
 
 
-def factor_kernel(n, pos_ref, own_ref, recv_ref, out_ref, fold, u_ref, strip, zref, turn, w_ref, uh, um, ul):
+def factor_kernel(n, pos_ref, own_ref, recv_ref, out_ref, fold, zref, turn, uh, um, ul):
     B = TILE
+    H = B // 2
     nb = n // B
     parts = (uh, um, ul)
     half = own_ref.shape[0]
@@ -237,46 +237,67 @@
         return 0
 
     lax.fori_loop(0, half, get, 0)
-    zref[...] = jnp.zeros((8, 128), f32)
-
-    def update(k):
-        right = slice(k * B, n)
-        panel, off = (k, 0) if k < nb // 2 else (nb - 1 - k, k + 1)
-        rows = fold[panel * B : (panel + 1) * B, off * B : (off + nb - k) * B]
-        if k:
-            cols = slice(k * B, (k + 1) * B)
-            rows = rows - mm6([u[: k * B, cols] for u in parts], [u[: k * B, right] for u in parts], 0, 0)
-        strip[:, right] = rows
-
-    def solve(k):
-        if k == nb - 1:
-            return
-        right = slice((k + 1) * B, n)
-        done = mm6(split(w_ref[...]), split(strip[:, right]), 1, 0)
-        u_ref[k * B : (k + 1) * B, right] = done
-        for u, v in zip(parts, split(done)):
-            u[k * B : (k + 1) * B, right] = v
-
-    def body(k, _):
-        for kk in range(nb):
-            pl.when(k == kk)(functools.partial(update, kk))
-        kc = pl.multiple_of(k * B, B)
-        U, W = factor128(strip[:, pl.ds(kc, B)], zref[...])
-        w_ref[...] = W
-        u_ref[pl.ds(kc, B), pl.ds(kc, B)] = U
-        for kk in range(nb):
-            pl.when(k == kk)(functools.partial(solve, kk))
-        return 0
-
-    lax.fori_loop(0, nb, body, 0)
+    zref[...] = jnp.zeros((8, B), f32)
+    lane = lax.broadcasted_iota(jnp.int32, (H, B), 1)
+    row = lax.broadcasted_iota(jnp.int32, (H, B), 0)
+    low = lane < H
+
+    def gram(k, j0, j1):
+        panel, off = (k, -k) if k < nb // 2 else (nb - 1 - k, 1)
+        return fold[panel * B : (panel + 1) * B, (j0 + off) * B : (j1 + off) * B]
+
+    def store(r, cols, value):
+        value = split(value)
+        for u, v in zip(parts, value):
+            u[r : r + H, cols] = v
+        return value
+
+    def under(value, top):
+        zero = jnp.zeros(value.shape, jnp.bfloat16)
+        return [jnp.concatenate([zero, v] if top else [v, zero], axis=0) for v in split(value)]
+
+    D = gram(0, 0, 1)
+    for k in range(nb):
+        r = k * B
+        here = slice(r, r + B)
+        rest = slice(r + B, n)
+        then = slice(r + B, r + 2 * B)
+        tail = k < nb - 1
+        X1, back1 = scaled(D[:H], 0, H)
+        if tail:
+            R = gram(k, k + 1, nb)
+            E = gram(k + 1, k + 1, k + 2)
+            if k:
+                R = R - mm6([u[:r, here] for u in parts], [u[:r, rest] for u in parts], 0, 0)
+                E = E - mm6([u[:r, then] for u in parts], [u[:r, then] for u in parts], 0, 0)
+        F1 = eliminate(X1, 0, zref[...]) * back1
+        f1 = split(F1)
+        U1 = mm6(f1, under(D[:H], True), 1, 0)
+        u12 = split(jnp.where(low, 0.0, U1))
+        D2 = D[H:] - mm6(u12, u12, 0, 0)[H:]
+        X2, back2 = scaled(D2, H, 0)
+        store(r, here, jnp.where(low, jnp.where(lane >= row, F1, 0.0), U1))
+        if tail:
+            P1 = mm6(f1, under(R[:H], True), 1, 0)
+            p1 = store(r, rest, P1)
+            R2 = R[H:] - mm6(u12, p1, 0, 0)[H:]
+            p1 = [v[:, :B] for v in p1]
+            E = E - mm6(p1, p1, 0, 0)
+        F2 = eliminate(X2, H, zref[...]) * back2
+        store(r + H, here, jnp.where(low | (lane - H < row), 0.0, F2))
+        if tail:
+            P2 = mm6(split(F2), under(R2, False), 1, 0)
+            p2 = [v[:, :B] for v in store(r + H, rest, P2)]
+            D = E - mm6(p2, p2, 0, 0)
     row_width, col_width = out_ref.shape
     first_row = pos_ref[1] * row_width
     first_col = pos_ref[2] * col_width
     lane_tile = pl.multiple_of(first_row // B * B, B)
     inner = pl.multiple_of(first_row % B, 8)
     for c in range(col_width // B):
-        block = u_ref[pl.ds(pl.multiple_of(first_col + c * B, B), B), pl.ds(lane_tile, B)]
-        turn[...] = block.T
+        where = (pl.ds(pl.multiple_of(first_col + c * B, B), B), pl.ds(lane_tile, B))
+        hi, mid, tiny = (u[where].astype(f32) for u in parts)
+        turn[...] = ((tiny + mid) + hi).T
         i = first_row + lax.broadcasted_iota(jnp.int32, (row_width, B), 0)
         j = first_col + c * B + lax.broadcasted_iota(jnp.int32, (row_width, B), 1)
         out_ref[:, c * B : (c + 1) * B] = jnp.where(j <= i, turn[pl.ds(inner, row_width), :], 0.0)
@@ -365,10 +386,7 @@
         out_specs=vmem,
         scratch_shapes=[
             pltpu.VMEM((fold_rows, fold_cols), f32),
-            pltpu.VMEM((n, n), f32),
-            pltpu.VMEM((TILE, n), f32),
-            pltpu.VMEM((8, 128), f32),
-            pltpu.VMEM((TILE, TILE), f32),
+            pltpu.VMEM((8, TILE), f32),
             pltpu.VMEM((TILE, TILE), f32),
         ]
         + [pltpu.VMEM((n, n), jnp.bfloat16)] * 3,

time: 153 us -> 142 us (0.928)
  Pallas kernels: 37.4 us -> 26.6 us
    pallas_call x1, Pallas kernels: 35.6 us -> 24.8 us  [local_fast(): pl.pallas_call(functools.partial(factor_kernel, n), out_shape=jax.ShapeDt...]
where the time goes in v3:
time: 142 us
  waiting for transfers between devices  84.2 us (59%)
  Pallas kernels  26.6 us (19%)
  starting transfers between devices  22.8 us (16%)
  matrix products  4.15 us (3%)
  other arithmetic  3.32 us (2%)
    all_to_all x1, waiting for transfers between devices, local_fast(): lax.all_to_all(local_mix, AXES, split_axis=0, concat_axis=0, tiled=True)  46.3 us
    ppermute x14, waiting for transfers between devices, xor_send(): return lax.ppermute(value, AXES, [(d, d ^ mask) for d in range(n_dev)])  37.9 us
    pallas_call x1, Pallas kernels, local_fast(): pl.pallas_call(functools.partial(factor_kernel, n), out_shape=jax.ShapeDt...  24.8 us
    ppermute x14, starting transfers between devices, xor_send(): return lax.ppermute(value, AXES, [(d, d ^ mask) for d in range(n_dev)])  15.4 us
    all_to_all x1, starting transfers between devices, local_fast(): lax.all_to_all(local_mix, AXES, split_axis=0, concat_axis=0, tiled=True)  7.32 us
    dot_general x1, matrix products, local_fast(): jnp.dot(hadamard(rows_dev, jnp.bfloat16), flipped, preferred_element_type...  4.15 us
  transfers between devices with their start and end apart: 15, of which 12 were waited for; matrix products, arithmetic and copies ran while one was open for 2% of the time, Pallas kernels for 0%

profile of v3, /device:TPU:0, one launch (start us, length us, event | category | flops | bytes accessed | tf_op | source)
XLA Modules:
  0.0 141.5 jit_solution(6712930647450657549)
XLA Ops:
  0.7 4.2 %fusion = f32[512,1024]{1,0:T(8,128)} fusion(bf16[512,1024]{1,0:T(8,128)(2,1)} %param.3, bf16[512]{0:T(512)(128)(2,1)S(1)} %subtract_convert_fusion.2), kind=kOutput, calls=%fused_computation.1 | convolution fusion | flops 545259520 | bytes 3146752 | tf_op jit(solution)/shard_map/dot_general | solution.py:323
  4.8 7.3 %all-to-all-start = ((f32[32,16,1024]{2,1,0:T(8,128)}), f32[32,16,1024]{2,1,0:T(8,128)S(1)}, u32[]{:S(2)}, u32[]{:S(2)}) async-start(f32[32,16,1024]{2,1,0:T(8,128)} %bitcast.4), calls=%async_computation | async-start | bytes 4194304 | tf_op jit(solution)/shard_map/all_to_all | solution.py:324
  12.3 2.3 %compare_reduce_fusion = pred[512]{0:T(512)(128)(4,1)S(1)} fusion(s32[8192]{0:T(1024)S(1)} %copy-done, s32[512]{0:T(512)S(1)} %fusion.24), kind=kLoop, calls=%fused_computation | loop fusion | flops 8388096 | bytes 35328 | tf_op jit(solution)/shard_map/reduce_or | solution.py:329
  14.5 46.3 %all-to-all-done.x_ref = f32[32,16,1024]{2,1,0:T(8,128)S(1)} async-done(((f32[32,16,1024]{2,1,0:T(8,128)}), f32[32,16,1024]{2,1,0:T(8,128)S(1)}, u32[]{:S(2)}, u32[]{:S(2)}) %all-to-all-start) | async-done | bytes 2097184 | tf_op jit(solution)/shard_map/all_to_all | solution.py:324
  61.0 1.8 %sketch_gram.1 = (f32[16,16,1152]{2,1,0:T(8,128)S(1)}, f32[16,16,1152]{2,1,0:T(8,128)S(1)}) custom-call(s32[1]{0:T(128)} %bitcast.me_ref, f32[32,16,1024]{2,1,0:T(8,128)S(1)} %all-to-all-done.x_ref, f32[512,128]{1,0:T(8,128)S(1)} %broadcast_in_dim.20.m_ref), custom_call_target="tpu_custom_call" | custom-call | tf_op jit(solution)/shard_map/sketch_gram/pallas_call | solution.py:352
  62.9 2.8 %collective-permute-done = f32[16,16,1152]{2,1,0:T(8,128)S(1)} collective-permute-done((f32[16,16,1152]{2,1,0:T(8,128)S(1)}, f32[16,16,1152]{2,1,0:T(8,128)S(1)}, u32[]{:S(2)}, u32[]{:S(2)}) %collective-permute-start) | collective-permute-done | bytes 1179680 | tf_op jit(solution)/shard_map/ppermute | solution.py:307
  65.9 1.5 %collective-permute-start.1 = (f32[4,16,1152]{2,1,0:T(8,128)S(1)}, f32[4,16,1152]{2,1,0:T(8,128)S(1)}, u32[]{:S(2)}, u32[]{:S(2)}) collective-permute-start(f32[4,16,1152]{2,1,0:T(8,128)S(1)} %get-tuple-element.11), channel_id=1, source_target_pairs={{0,4},{1,5},{2,6},{3,7},{4,0},{5,1},{6,2},{7,3},{8,12},{9,13},{10,... | collective-permute-start | bytes 884744 | tf_op jit(solution)/shard_map/ppermute | solution.py:307
  67.5 1.6 %collective-permute-start.3 = (f32[4,16,1152]{2,1,0:T(8,128)S(1)}, f32[4,16,1152]{2,1,0:T(8,128)S(1)}, u32[]{:S(2)}, u32[]{:S(2)}) collective-permute-start(f32[4,16,1152]{2,1,0:T(8,128)S(1)} %get-tuple-element.12), channel_id=1, source_target_pairs={{0,5},{1,4},{2,7},{3,6},{4,1},{5,0},{6,3},{7,2},{8,13},{9,12},{10,... | collective-permute-start | bytes 884744 | tf_op jit(solution)/shard_map/ppermute | solution.py:307
  69.5 6.4 %collective-permute-done.1 = f32[4,16,1152]{2,1,0:T(8,128)S(1)} collective-permute-done((f32[4,16,1152]{2,1,0:T(8,128)S(1)}, f32[4,16,1152]{2,1,0:T(8,128)S(1)}, u32[]{:S(2)}, u32[]{:S(2)}) %collective-permute-start.1) | collective-permute-done | bytes 294944 | tf_op jit(solution)/shard_map/ppermute | solution.py:307
  75.9 6.7 %collective-permute-done.3 = f32[4,16,1152]{2,1,0:T(8,128)S(1)} collective-permute-done((f32[4,16,1152]{2,1,0:T(8,128)S(1)}, f32[4,16,1152]{2,1,0:T(8,128)S(1)}, u32[]{:S(2)}, u32[]{:S(2)}) %collective-permute-start.3) | collective-permute-done | bytes 294944 | tf_op jit(solution)/shard_map/ppermute | solution.py:307
  82.5 1.4 collective-permute-done.2
  85.6 2.0 %collective-permute-start.5 = (f32[1,16,1152]{2,1,0:T(8,128)S(1)}, f32[1,16,1152]{2,1,0:T(8,128)S(1)}, u32[]{:S(2)}, u32[]{:S(2)}) collective-permute-start(f32[1,16,1152]{2,1,0:T(8,128)S(1)} %get-tuple-element.16), channel_id=1, source_target_pairs={{0,16},{1,17},{2,18},{3,19},{4,20},{5,21},{6,22},{7,23},{8,24},{9,... | collective-permute-start | bytes 221192 | tf_op jit(solution)/shard_map/ppermute | solution.py:307
  87.5 1.4 collective-permute-done.4
  88.9 1.8 %collective-permute-done.6 = f32[1,16,1152]{2,1,0:T(8,128)S(1)} collective-permute-done((f32[1,16,1152]{2,1,0:T(8,128)S(1)}, f32[1,16,1152]{2,1,0:T(8,128)S(1)}, u32[]{:S(2)}, u32[]{:S(2)}) %collective-permute-start.6) | collective-permute-done | bytes 73760 | tf_op jit(solution)/shard_map/ppermute | solution.py:307
  90.7 2.2 %collective-permute-done.5 = f32[1,16,1152]{2,1,0:T(8,128)S(1)} collective-permute-done((f32[1,16,1152]{2,1,0:T(8,128)S(1)}, f32[1,16,1152]{2,1,0:T(8,128)S(1)}, u32[]{:S(2)}, u32[]{:S(2)}) %collective-permute-start.5) | collective-permute-done | bytes 73760 | tf_op jit(solution)/shard_map/ppermute | solution.py:307
  93.0 2.2 %collective-permute-start.9 = (f32[1,16,1152]{2,1,0:T(8,128)S(1)}, f32[1,16,1152]{2,1,0:T(8,128)S(1)}, u32[]{:S(2)}, u32[]{:S(2)}) collective-permute-start(f32[1,16,1152]{2,1,0:T(8,128)S(1)} %get-tuple-element.10), channel_id=1, source_target_pairs={{0,24},{1,25},{2,26},{3,27},{4,28},{5,29},{6,30},{7,31},{8,16},{9,... | collective-permute-start | bytes 221192 | tf_op jit(solution)/shard_map/ppermute | solution.py:307
  95.1 2.3 %collective-permute-start.7 = (f32[1,16,1152]{2,1,0:T(8,128)S(1)}, f32[1,16,1152]{2,1,0:T(8,128)S(1)}, u32[]{:S(2)}, u32[]{:S(2)}) collective-permute-start(f32[1,16,1152]{2,1,0:T(8,128)S(1)} %get-tuple-element.10), channel_id=1, source_target_pairs={{0,8},{1,9},{2,10},{3,11},{4,12},{5,13},{6,14},{7,15},{8,0},{9,1},... | collective-permute-start | bytes 221192 | tf_op jit(solution)/shard_map/ppermute | solution.py:307
  97.4 1.8 %collective-permute-done.9 = f32[1,16,1152]{2,1,0:T(8,128)S(1)} collective-permute-done((f32[1,16,1152]{2,1,0:T(8,128)S(1)}, f32[1,16,1152]{2,1,0:T(8,128)S(1)}, u32[]{:S(2)}, u32[]{:S(2)}) %collective-permute-start.9) | collective-permute-done | bytes 73760 | tf_op jit(solution)/shard_map/ppermute | solution.py:307
  99.2 1.6 %collective-permute-done.8 = f32[1,16,1152]{2,1,0:T(8,128)S(1)} collective-permute-done((f32[1,16,1152]{2,1,0:T(8,128)S(1)}, f32[1,16,1152]{2,1,0:T(8,128)S(1)}, u32[]{:S(2)}, u32[]{:S(2)}) %collective-permute-start.8) | collective-permute-done | bytes 73760 | tf_op jit(solution)/shard_map/ppermute | solution.py:307
  100.8 1.9 %collective-permute-start.12 = (f32[4,16,1152]{2,1,0:T(8,128)S(1)}, f32[4,16,1152]{2,1,0:T(8,128)S(1)}, u32[]{:S(2)}, u32[]{:S(2)}) collective-permute-start(f32[4,16,1152]{2,1,0:T(8,128)S(1)} %pad_maximum_fusion), channel_id=1, source_target_pairs={{0,5},{1,4},{2,7},{3,6},{4,1},{5,0},{6,3},{7,2},{8,13},{9,12},{10,... | collective-permute-start | bytes 884744 | tf_op jit(solution)/shard_map/ppermute | solution.py:307
  102.7 1.8 %collective-permute-start.11 = (f32[4,16,1152]{2,1,0:T(8,128)S(1)}, f32[4,16,1152]{2,1,0:T(8,128)S(1)}, u32[]{:S(2)}, u32[]{:S(2)}) collective-permute-start(f32[4,16,1152]{2,1,0:T(8,128)S(1)} %pad_maximum_fusion), channel_id=1, source_target_pairs={{0,1},{1,0},{2,3},{3,2},{4,5},{5,4},{6,7},{7,6},{8,9},{9,8},{10,11... | collective-permute-start | bytes 884744 | tf_op jit(solution)/shard_map/ppermute | solution.py:307
  104.6 9.1 %collective-permute-done.10 = f32[4,16,1152]{2,1,0:T(8,128)S(1)} collective-permute-done((f32[4,16,1152]{2,1,0:T(8,128)S(1)}, f32[4,16,1152]{2,1,0:T(8,128)S(1)}, u32[]{:S(2)}, u32[]{:S(2)}) %collective-permute-start.10) | collective-permute-done | bytes 294944 | tf_op jit(solution)/shard_map/ppermute | solution.py:307
  113.9 2.8 %collective-permute-done.13.recv_ref = f32[16,16,1152]{2,1,0:T(8,128)S(1)} collective-permute-done((f32[16,16,1152]{2,1,0:T(8,128)S(1)}, f32[16,16,1152]{2,1,0:T(8,128)S(1)}, u32[]{:S(2)}, u32[]{:S(2)}) %collective-permute-start.13) | collective-permute-done | bytes 1179680 | tf_op jit(solution)/shard_map/ppermute | solution.py:307
  116.7 24.8 %factor.1 = f32[64,512]{1,0:T(8,128)} custom-call(s32[3]{0:T(128)S(1)} %pad_add_fusion.pos_ref, f32[16,16,1152]{2,1,0:T(8,128)S(1)} %constant_dynamic-update-slice_fusion.own_ref, f32[16,16,1152]{2,1,0:T(8,128)S(1)} %collective-permute-done.13.recv_ref), custom_call_target="tpu_custom_call" | custom-call | tf_op jit(solution)/shard_map/factor/pallas_call | solution.py:382
  (29 shorter events, 3.4 us)
Async XLA Ops:
  4.8 7.4 %copy-start = (s32[8192]{0:T(1024)S(1)}, s32[8192]{0:T(1024)}, u32[]{:S(2)}) copy-start(s32[8192]{0:T(1024)} %param.5) | copy-start | bytes 98308
  4.8 56.0 %all-to-all-start = ((f32[32,16,1024]{2,1,0:T(8,128)}), f32[32,16,1024]{2,1,0:T(8,128)S(1)}, u32[]{:S(2)}, u32[]{:S(2)}) async-start(f32[32,16,1024]{2,1,0:T(8,128)} %bitcast.4), calls=%async_computation | async-start | bytes 4194304 | tf_op jit(solution)/shard_map/all_to_all | solution.py:324
  62.8 2.9 %collective-permute-start = (f32[16,16,1152]{2,1,0:T(8,128)S(1)}, f32[16,16,1152]{2,1,0:T(8,128)S(1)}, u32[]{:S(2)}, u32[]{:S(2)}) collective-permute-start(f32[16,16,1152]{2,1,0:T(8,128)S(1)} %get-tuple-element.8), channel_id=1, source_target_pairs={{0,2},{1,3},{2,0},{3,1},{4,6},{5,7},{6,4},{7,5},{8,10},{9,11},{10,... | collective-permute-start | bytes 3538952 | tf_op jit(solution)/shard_map/ppermute | solution.py:307
  65.9 9.9 %collective-permute-start.1 = (f32[4,16,1152]{2,1,0:T(8,128)S(1)}, f32[4,16,1152]{2,1,0:T(8,128)S(1)}, u32[]{:S(2)}, u32[]{:S(2)}) collective-permute-start(f32[4,16,1152]{2,1,0:T(8,128)S(1)} %get-tuple-element.11), channel_id=1, source_target_pairs={{0,4},{1,5},{2,6},{3,7},{4,0},{5,1},{6,2},{7,3},{8,12},{9,13},{10,... | collective-permute-start | bytes 884744 | tf_op jit(solution)/shard_map/ppermute | solution.py:307
  67.5 15.1 %collective-permute-start.3 = (f32[4,16,1152]{2,1,0:T(8,128)S(1)}, f32[4,16,1152]{2,1,0:T(8,128)S(1)}, u32[]{:S(2)}, u32[]{:S(2)}) collective-permute-start(f32[4,16,1152]{2,1,0:T(8,128)S(1)} %get-tuple-element.12), channel_id=1, source_target_pairs={{0,5},{1,4},{2,7},{3,6},{4,1},{5,0},{6,3},{7,2},{8,13},{9,12},{10,... | collective-permute-start | bytes 884744 | tf_op jit(solution)/shard_map/ppermute | solution.py:307
  69.1 14.8 %collective-permute-start.2 = (f32[4,16,1152]{2,1,0:T(8,128)S(1)}, f32[4,16,1152]{2,1,0:T(8,128)S(1)}, u32[]{:S(2)}, u32[]{:S(2)}) collective-permute-start(f32[4,16,1152]{2,1,0:T(8,128)S(1)} %get-tuple-element.13), channel_id=1, source_target_pairs={{0,1},{1,0},{2,3},{3,2},{4,5},{5,4},{6,7},{7,6},{8,9},{9,8},{10,11... | collective-permute-start | bytes 884744 | tf_op jit(solution)/shard_map/ppermute | solution.py:307
  84.0 4.9 %collective-permute-start.4 = (f32[1,16,1152]{2,1,0:T(8,128)S(1)}, f32[1,16,1152]{2,1,0:T(8,128)S(1)}, u32[]{:S(2)}, u32[]{:S(2)}) collective-permute-start(f32[1,16,1152]{2,1,0:T(8,128)S(1)} %get-tuple-element.14), channel_id=1, source_target_pairs={{0,8},{1,9},{2,10},{3,11},{4,12},{5,13},{6,14},{7,15},{8,0},{9,1},... | collective-permute-start | bytes 221192 | tf_op jit(solution)/shard_map/ppermute | solution.py:307
  84.5 6.2 %collective-permute-start.6 = (f32[1,16,1152]{2,1,0:T(8,128)S(1)}, f32[1,16,1152]{2,1,0:T(8,128)S(1)}, u32[]{:S(2)}, u32[]{:S(2)}) collective-permute-start(f32[1,16,1152]{2,1,0:T(8,128)S(1)} %get-tuple-element.15), channel_id=1, source_target_pairs={{0,24},{1,25},{2,26},{3,27},{4,28},{5,29},{6,30},{7,31},{8,16},{9,... | collective-permute-start | bytes 221192 | tf_op jit(solution)/shard_map/ppermute | solution.py:307
  85.6 7.4 %collective-permute-start.5 = (f32[1,16,1152]{2,1,0:T(8,128)S(1)}, f32[1,16,1152]{2,1,0:T(8,128)S(1)}, u32[]{:S(2)}, u32[]{:S(2)}) collective-permute-start(f32[1,16,1152]{2,1,0:T(8,128)S(1)} %get-tuple-element.16), channel_id=1, source_target_pairs={{0,16},{1,17},{2,18},{3,19},{4,20},{5,21},{6,22},{7,23},{8,24},{9,... | collective-permute-start | bytes 221192 | tf_op jit(solution)/shard_map/ppermute | solution.py:307
  93.0 6.2 %collective-permute-start.9 = (f32[1,16,1152]{2,1,0:T(8,128)S(1)}, f32[1,16,1152]{2,1,0:T(8,128)S(1)}, u32[]{:S(2)}, u32[]{:S(2)}) collective-permute-start(f32[1,16,1152]{2,1,0:T(8,128)S(1)} %get-tuple-element.10), channel_id=1, source_target_pairs={{0,24},{1,25},{2,26},{3,27},{4,28},{5,29},{6,30},{7,31},{8,16},{9,... | collective-permute-start | bytes 221192 | tf_op jit(solution)/shard_map/ppermute | solution.py:307
  95.1 5.6 %collective-permute-start.8 = (f32[1,16,1152]{2,1,0:T(8,128)S(1)}, f32[1,16,1152]{2,1,0:T(8,128)S(1)}, u32[]{:S(2)}, u32[]{:S(2)}) collective-permute-start(f32[1,16,1152]{2,1,0:T(8,128)S(1)} %get-tuple-element.10), channel_id=1, source_target_pairs={{0,16},{1,17},{2,18},{3,19},{4,20},{5,21},{6,22},{7,23},{8,24},{9,... | collective-permute-start | bytes 221192 | tf_op jit(solution)/shard_map/ppermute | solution.py:307
  95.1 5.6 %collective-permute-start.7 = (f32[1,16,1152]{2,1,0:T(8,128)S(1)}, f32[1,16,1152]{2,1,0:T(8,128)S(1)}, u32[]{:S(2)}, u32[]{:S(2)}) collective-permute-start(f32[1,16,1152]{2,1,0:T(8,128)S(1)} %get-tuple-element.10), channel_id=1, source_target_pairs={{0,8},{1,9},{2,10},{3,11},{4,12},{5,13},{6,14},{7,15},{8,0},{9,1},... | collective-permute-start | bytes 221192 | tf_op jit(solution)/shard_map/ppermute | solution.py:307
  100.8 13.0 %collective-permute-start.12 = (f32[4,16,1152]{2,1,0:T(8,128)S(1)}, f32[4,16,1152]{2,1,0:T(8,128)S(1)}, u32[]{:S(2)}, u32[]{:S(2)}) collective-permute-start(f32[4,16,1152]{2,1,0:T(8,128)S(1)} %pad_maximum_fusion), channel_id=1, source_target_pairs={{0,5},{1,4},{2,7},{3,6},{4,1},{5,0},{6,3},{7,2},{8,13},{9,12},{10,... | collective-permute-start | bytes 884744 | tf_op jit(solution)/shard_map/ppermute | solution.py:307
  102.7 11.0 %collective-permute-start.11 = (f32[4,16,1152]{2,1,0:T(8,128)S(1)}, f32[4,16,1152]{2,1,0:T(8,128)S(1)}, u32[]{:S(2)}, u32[]{:S(2)}) collective-permute-start(f32[4,16,1152]{2,1,0:T(8,128)S(1)} %pad_maximum_fusion), channel_id=1, source_target_pairs={{0,1},{1,0},{2,3},{3,2},{4,5},{5,4},{6,7},{7,6},{8,9},{9,8},{10,11... | collective-permute-start | bytes 884744 | tf_op jit(solution)/shard_map/ppermute | solution.py:307
  104.5 9.2 %collective-permute-start.10 = (f32[4,16,1152]{2,1,0:T(8,128)S(1)}, f32[4,16,1152]{2,1,0:T(8,128)S(1)}, u32[]{:S(2)}, u32[]{:S(2)}) collective-permute-start(f32[4,16,1152]{2,1,0:T(8,128)S(1)} %pad_maximum_fusion), channel_id=1, source_target_pairs={{0,4},{1,5},{2,6},{3,7},{4,0},{5,1},{6,2},{7,3},{8,12},{9,13},{10,... | collective-permute-start | bytes 884744 | tf_op jit(solution)/shard_map/ppermute | solution.py:307
  113.8 2.9 %collective-permute-start.13 = (f32[16,16,1152]{2,1,0:T(8,128)S(1)}, f32[16,16,1152]{2,1,0:T(8,128)S(1)}, u32[]{:S(2)}, u32[]{:S(2)}) collective-permute-start(f32[16,16,1152]{2,1,0:T(8,128)S(1)} %constant_dynamic-update-slice_fusion.own_ref), channel_id=1, source_target_pairs={{0,2},{1,3},{2,0},{3,1},{4,6},{5,7},{6,4},{7,5},{8,10},{9,11},{10,... | collective-permute-start | bytes 3538952 | tf_op jit(solution)/shard_map/ppermute | solution.py:307

commit v4 on v3

--- a/solution.py
+++ b/solution.py
@@ -176,7 +176,55 @@
     return X, jnp.where(half[0:1], across * root, 1.0)
 
 
-def sketch_gram_kernel(n_dev, me_ref, x_ref, m_ref, keep_ref, send_ref, s_ref, fold):
+def local_kernel(sign_ref, panel_ref, out_ref, signed):
+    blocks = panel_ref.shape[0] // TILE
+
+    @pl.when(pl.program_id(0) == 0)
+    def _():
+        table = hadamard(TILE, f32)
+        for b in range(blocks):
+            sign = 1 - 2 * sign_ref[:, b * TILE : (b + 1) * TILE]
+            signed[b] = (table * sign.astype(f32)).astype(jnp.bfloat16)
+
+    v = [
+        jnp.dot(signed[b], panel_ref[b * TILE : (b + 1) * TILE, :], preferred_element_type=f32) for b in range(blocks)
+    ]
+    h = 1
+    while h < blocks:
+        w = list(v)
+        for b in range(blocks):
+            if not b & h:
+                w[b] = v[b] + v[b | h]
+                w[b | h] = v[b] - v[b | h]
+        v = w
+        h *= 2
+    for b in range(blocks):
+        out_ref[b * TILE : (b + 1) * TILE, :] = v[b]
+
+
+def cells_of(nb):
+    cells = []
+    for k in range(nb):
+        cells.append(("top", k))
+        cells += [("full", k, j, i) for j in range(k + 1, nb) for i in range(2)]
+        if k % 2 == 0:
+            cells.append(("low", k // 2))
+    return cells
+
+
+def head_tiles(nb, panels, deep):
+    cells = cells_of(nb)
+    need = [c for c in cells if c[1] < panels and c[0] != "low" or c[0] == "low" and 2 * c[1] < panels]
+    return -(-(1 + max(cells.index(c) for c in need)) // deep)
+
+
+def slot(nb, deep, cell):
+    at = cells_of(nb).index(cell)
+    half = TILE // 2
+    return slice(at % deep * half, (at % deep + 1) * half), slice(at // deep * TILE, (at // deep + 1) * TILE)
+
+
+def sketch_gram_kernel(n_dev, me_ref, x_ref, m_ref, keep_ref, send_ref, s_ref, pack):
     n = x_ref.shape[2]
     nb = n // TILE
     per = x_ref.shape[1]
@@ -201,6 +249,10 @@
         return 0
 
     lax.fori_loop(0, nb, mix, 0)
+    H = TILE // 2
+    deep = pack.shape[0] // H
+    lane = lax.broadcasted_iota(jnp.int32, (H, TILE), 1)
+    even = None
     for k in range(nb):
         part = lax.dot_general(
             s_ref[:, k * TILE : (k + 1) * TILE],
@@ -208,32 +260,50 @@
             TA,
             preferred_element_type=f32,
         )
-        panel, off = (k, 0) if k < nb // 2 else (nb - 1 - k, k + 1)
-        fold[panel * TILE : (panel + 1) * TILE, off * TILE : (off + nb - k) * TILE] = part
+        pack[slot(nb, deep, ("top", k))] = part[:H, :TILE]
+        for j in range(k + 1, nb):
+            for i in range(2):
+                cols = slice((j - k) * TILE, (j - k + 1) * TILE)
+                pack[slot(nb, deep, ("full", k, j, i))] = part[i * H : (i + 1) * H, cols]
+        if k % 2 == 0:
+            even = part[H:, :TILE]
+        else:
+            odd = pltpu.roll(part[H:, :TILE], H, 1)
+            pack[slot(nb, deep, ("low", k // 2))] = jnp.where(lane < H, odd, even)
     half = n_dev // 2
     me = me_ref[0]
     h = keep_ref.shape[1]
 
     def put(j, _):
-        keep_ref[j] = fold[pl.ds(pl.multiple_of((j ^ me) * h, 8), h), :]
-        send_ref[j] = fold[pl.ds(pl.multiple_of(((j + half) ^ me) * h, 8), h), :]
+        keep_ref[j] = pack[pl.ds(pl.multiple_of((j ^ me) * h, 8), h), :]
+        send_ref[j] = pack[pl.ds(pl.multiple_of(((j + half) ^ me) * h, 8), h), :]
         return 0
 
     lax.fori_loop(0, half, put, 0)
 
 
-def factor_kernel(n, pos_ref, own_ref, recv_ref, out_ref, fold, zref, turn, uh, um, ul):
+def factor_kernel(n, p0, p1, head, pos_ref, own_ref, recv_ref, *refs):
+    refs = list(refs)
+    last = p1 == n // TILE
+    old = [refs.pop(0) for _ in range(3)] if p0 else None
+    kept = refs.pop(0) if p0 else None
+    if last:
+        out_ref = refs.pop(0)
+        parts = refs[-3:]
+    else:
+        parts = [refs.pop(0) for _ in range(3)]
+        keep_ref = refs.pop(0)
+    pack, zref, turn = refs[:3]
     B = TILE
     H = B // 2
     nb = n // B
-    parts = (uh, um, ul)
     half = own_ref.shape[0]
     h = own_ref.shape[1]
     me = pos_ref[0]
 
     def get(j, _):
-        fold[pl.ds(pl.multiple_of((j ^ me) * h, 8), h), :] = own_ref[j]
-        fold[pl.ds(pl.multiple_of(((j + half) ^ me) * h, 8), h), :] = recv_ref[j]
+        pack[pl.ds(pl.multiple_of((j ^ me) * h, 8), h), :] = own_ref[j]
+        pack[pl.ds(pl.multiple_of(((j + half) ^ me) * h, 8), h), :] = recv_ref[j]
         return 0
 
     lax.fori_loop(0, half, get, 0)
@@ -242,22 +312,46 @@
     row = lax.broadcasted_iota(jnp.int32, (H, B), 0)
     low = lane < H
 
-    def gram(k, j0, j1):
-        panel, off = (k, -k) if k < nb // 2 else (nb - 1 - k, 1)
-        return fold[panel * B : (panel + 1) * B, (j0 + off) * B : (j1 + off) * B]
+    deep = pack.shape[0] // H
+
+    def cell(*name):
+        rows, lanes = slot(nb, deep, name)
+        if p0 and lanes.start < head * B:
+            return kept[rows, lanes.start - (head - 1) * B : lanes.stop - (head - 1) * B]
+        base = head * B if p0 else 0
+        return pack[rows, lanes.start - base : lanes.stop - base]
+
+    def diagonal(k):
+        low_part = cell("low", k // 2)
+        return jnp.concatenate([cell("top", k), pltpu.roll(low_part, H, 1) if k % 2 else low_part], axis=0)
+
+    def beside(k):
+        rows = [jnp.concatenate([cell("full", k, j, i) for j in range(k + 1, nb)], axis=1) for i in range(2)]
+        return jnp.concatenate(rows, axis=0)
+
+    def above(k, cols):
+        new = [u[: (k - p0) * B, cols] for u in parts]
+        if not p0:
+            return new
+        if k == p0:
+            return [u[:, cols] for u in old]
+        return [jnp.concatenate([o[:, cols], u], axis=0) for o, u in zip(old, new)]
 
     def store(r, cols, value):
         value = split(value)
         for u, v in zip(parts, value):
-            u[r : r + H, cols] = v
+            u[r - p0 * B : r - p0 * B + H, cols] = v
         return value
 
     def under(value, top):
         zero = jnp.zeros(value.shape, jnp.bfloat16)
         return [jnp.concatenate([zero, v] if top else [v, zero], axis=0) for v in split(value)]
 
-    D = gram(0, 0, 1)
-    for k in range(nb):
+    D = diagonal(p0)
+    if p0:
+        left = above(p0, slice(p0 * B, (p0 + 1) * B))
+        D = D - mm6(left, left, 0, 0)
+    for k in range(p0, p1):
         r = k * B
         here = slice(r, r + B)
         rest = slice(r + B, n)
@@ -265,11 +359,14 @@
         tail = k < nb - 1
         X1, back1 = scaled(D[:H], 0, H)
         if tail:
-            R = gram(k, k + 1, nb)
-            E = gram(k + 1, k + 1, k + 2)
+            R = beside(k)
             if k:
-                R = R - mm6([u[:r, here] for u in parts], [u[:r, rest] for u in parts], 0, 0)
-                E = E - mm6([u[:r, then] for u in parts], [u[:r, then] for u in parts], 0, 0)
+                R = R - mm6(above(k, here), above(k, rest), 0, 0)
+            if k < p1 - 1:
+                E = diagonal(k + 1)
+                if k:
+                    left = above(k, then)
+                    E = E - mm6(left, left, 0, 0)
         F1 = eliminate(X1, 0, zref[...]) * back1
         f1 = split(F1)
         U1 = mm6(f1, under(D[:H], True), 1, 0)
@@ -279,25 +376,37 @@
         store(r, here, jnp.where(low, jnp.where(lane >= row, F1, 0.0), U1))
         if tail:
             P1 = mm6(f1, under(R[:H], True), 1, 0)
-            p1 = store(r, rest, P1)
-            R2 = R[H:] - mm6(u12, p1, 0, 0)[H:]
-            p1 = [v[:, :B] for v in p1]
-            E = E - mm6(p1, p1, 0, 0)
+            first = store(r, rest, P1)
+            R2 = R[H:] - mm6(u12, first, 0, 0)[H:]
+            if k < p1 - 1:
+                first = [v[:, :B] for v in first]
+                E = E - mm6(first, first, 0, 0)
         F2 = eliminate(X2, H, zref[...]) * back2
         store(r + H, here, jnp.where(low | (lane - H < row), 0.0, F2))
         if tail:
             P2 = mm6(split(F2), under(R2, False), 1, 0)
-            p2 = [v[:, :B] for v in store(r + H, rest, P2)]
-            D = E - mm6(p2, p2, 0, 0)
+            second = [v[:, :B] for v in store(r + H, rest, P2)]
+            if k < p1 - 1:
+                D = E - mm6(second, second, 0, 0)
+    if not last:
+        keep_ref[...] = pack[:, (head - 1) * B :]
+        return
     row_width, col_width = out_ref.shape
     first_row = pos_ref[1] * row_width
     first_col = pos_ref[2] * col_width
     lane_tile = pl.multiple_of(first_row // B * B, B)
     inner = pl.multiple_of(first_row % B, 8)
     for c in range(col_width // B):
-        where = (pl.ds(pl.multiple_of(first_col + c * B, B), B), pl.ds(lane_tile, B))
-        hi, mid, tiny = (u[where].astype(f32) for u in parts)
-        turn[...] = ((tiny + mid) + hi).T
+        rb = first_col // B + c
+
+        def take(src, block):
+            where = (pl.ds(pl.multiple_of(block * B, B), B), pl.ds(lane_tile, B))
+            hi, mid, tiny = (u[where].astype(f32) for u in src)
+            turn[...] = ((tiny + mid) + hi).T
+
+        if p0:
+            pl.when(rb < p0)(lambda: take(old, jnp.minimum(rb, p0 - 1)))
+        pl.when(rb >= p0)(lambda: take(parts, jnp.clip(rb - p0, 0, nb - p0 - 1)))
         i = first_row + lax.broadcasted_iota(jnp.int32, (row_width, B), 0)
         j = first_col + c * B + lax.broadcasted_iota(jnp.int32, (row_width, B), 1)
         out_ref[:, c * B : (c + 1) * B] = jnp.where(j <= i, turn[pl.ds(inner, row_width), :], 0.0)
@@ -319,8 +428,22 @@
     grp_i = lax.axis_index("grp")
     lin = row_i * n_grp + grp_i
 
-    flipped = panel_rows * (1 - 2 * sign_bits).astype(jnp.bfloat16)[:, None]
-    local_mix = jnp.dot(hadamard(rows_dev, jnp.bfloat16), flipped, preferred_element_type=f32)
+    vmem = pl.BlockSpec(memory_space=pltpu.VMEM)
+    smem = pl.BlockSpec(memory_space=pltpu.SMEM)
+    width = 2 * TILE
+    local_mix = pl.pallas_call(
+        local_kernel,
+        grid=(n // width,),
+        out_shape=jax.ShapeDtypeStruct((rows_dev, n), f32),
+        in_specs=[
+            pl.BlockSpec((1, rows_dev), lambda c: (0, 0)),
+            pl.BlockSpec((rows_dev, width), lambda c: (0, c)),
+        ],
+        out_specs=pl.BlockSpec((rows_dev, width), lambda c: (0, c)),
+        scratch_shapes=[pltpu.VMEM((rows_dev // TILE, TILE, TILE), jnp.bfloat16)],
+        compiler_params=pltpu.CompilerParams(vmem_limit_bytes=60 << 20),
+        name="local_mix",
+    )(sign_bits[None], panel_rows)
     mixed = lax.all_to_all(local_mix, AXES, split_axis=0, concat_axis=0, tiled=True)
     mixed = mixed.reshape(n_dev, per, n)
 
@@ -342,19 +465,17 @@
         return sum(bit for pos, bit in enumerate(stage) if step >> pos & 1)
 
     nb = n // TILE
-    fold_rows = nb // 2 * TILE
-    fold_cols = (nb + 1) * TILE
-    h = fold_rows // n_dev
+    rows = 8 * n_dev
+    deep = rows // (TILE // 2)
+    lanes = -(-len(cells_of(nb)) // deep) * TILE
     half = n_dev // 2
-    piece = jax.ShapeDtypeStruct((half, h, fold_cols), f32)
-    vmem = pl.BlockSpec(memory_space=pltpu.VMEM)
-    smem = pl.BlockSpec(memory_space=pltpu.SMEM)
+    piece = jax.ShapeDtypeStruct((half, 8, lanes), f32)
     keep, send = pl.pallas_call(
         functools.partial(sketch_gram_kernel, n_dev),
         out_shape=(piece, piece),
         in_specs=[smem, vmem, vmem],
         out_specs=(vmem, vmem),
-        scratch_shapes=[pltpu.VMEM((rows_dev, n), jnp.bfloat16), pltpu.VMEM((fold_rows, fold_cols), f32)],
+        scratch_shapes=[pltpu.VMEM((rows_dev, n), jnp.bfloat16), pltpu.VMEM((rows, lanes), f32)],
         compiler_params=pltpu.CompilerParams(vmem_limit_bytes=40 << 20),
         name="sketch_gram",
     )(place[None], mixed, weight)
@@ -364,35 +485,56 @@
         ways = 1 << len(stage)
         if ways == 1:
             continue
-        parts = total.reshape(ways, total.shape[0] // ways, h, fold_cols)
+        parts = total.reshape(ways, total.shape[0] // ways, 8, lanes)
         got = [xor_send(parts[s], mask_of(stage, s), n_dev) for s in range(1, ways)]
         total = parts[0]
         for g in got:
             total = total + g
-    for stage in reversed(stages[1:]):
+
+    def spread(total, stage):
         ways = 1 << len(stage)
-        if ways == 1:
-            continue
         got = [xor_send(total, mask_of(stage, s), n_dev) for s in range(1, ways)]
-        total = jnp.concatenate([total] + got, axis=0)
-    other = xor_send(total, mask_of(stages[0], 1), n_dev)
+        return jnp.concatenate([total] + got, axis=0) if got else total
 
     row_width = n // n_row
     col_width = n // n_grp
-    return pl.pallas_call(
-        functools.partial(factor_kernel, n),
-        out_shape=jax.ShapeDtypeStruct((row_width, col_width), f32),
-        in_specs=[smem, vmem, vmem],
-        out_specs=vmem,
-        scratch_shapes=[
-            pltpu.VMEM((fold_rows, fold_cols), f32),
-            pltpu.VMEM((8, TILE), f32),
-            pltpu.VMEM((TILE, TILE), f32),
-        ]
-        + [pltpu.VMEM((n, n), jnp.bfloat16)] * 3,
-        compiler_params=pltpu.CompilerParams(vmem_limit_bytes=40 << 20),
-        name="factor",
-    )(jnp.stack([place, row_i, grp_i]), total, other)
+    cuts = [0, nb]
+    tiles = head_tiles(nb, cuts[1], deep) if len(cuts) > 2 else 0
+
+    def factor(p0, p1, own, state):
+        last = p1 == nb
+        store = [((p1 - p0) * TILE, n)] * 3
+        work = 8 * 2 * n * n * TILE * (p1 - p0)
+        return pl.pallas_call(
+            functools.partial(factor_kernel, n, p0, p1, tiles),
+            out_shape=(
+                (jax.ShapeDtypeStruct((row_width, col_width), f32),)
+                if last
+                else tuple(jax.ShapeDtypeStruct(d, jnp.bfloat16) for d in store)
+                + (jax.ShapeDtypeStruct((rows, TILE), f32),)
+            ),
+            in_specs=[smem] + [vmem] * (2 + len(state)),
+            out_specs=(vmem,) * (1 if last else 4),
+            scratch_shapes=[
+                pltpu.VMEM((rows, own[0].shape[2]), f32),
+                pltpu.VMEM((8, TILE), f32),
+                pltpu.VMEM((TILE, TILE), f32),
+            ]
+            + ([pltpu.VMEM(d, jnp.bfloat16) for d in store] if last else []),
+            compiler_params=pltpu.CompilerParams(vmem_limit_bytes=40 << 20),
+            cost_estimate=pl.CostEstimate(flops=work, bytes_accessed=1 << 20, transcendentals=0),
+            name="factor",
+        )(jnp.stack([place, row_i, grp_i]), *own, *state)
+
+    total = spread(total, stages[2])
+    split_lanes = [0] + [tiles * TILE] * (len(cuts) > 2) + [lanes]
+    shares = [spread(total[:, :, lo:hi], stages[1]) for lo, hi in zip(split_lanes, split_lanes[1:])]
+    state = ()
+    for p0, p1, share in zip(cuts, cuts[1:], shares):
+        if state:
+            share, state = lax.optimization_barrier((share, state))
+        state = factor(p0, p1, (share, xor_send(share, mask_of(stages[0], 1), n_dev)), state)
+    return state[0]
 
 
 def local(panel_rows, sign_bits, sample_rows):
@@ -403,10 +545,12 @@
     fits = (
         n % (2 * TILE) == 0
         and n_dev & (n_dev - 1) == 0
+        and rows_dev & (rows_dev - 1) == 0
+        and rows_dev % TILE == 0
         and 2 <= n_row
         and n_dev <= 64
         and rows_dev % (8 * n_dev) == 0
-        and n // 2 % (8 * n_dev) == 0
+        and n_dev % 8 == 0
         and TILE % (n // n_row) == 0
         and n // n_row % 8 == 0
         and n // n_grp % TILE == 0

time: 142 us -> 139 us (0.979)
  Pallas kernels: 26.6 us -> 31.1 us
  matrix products: 4.15 us -> 0 us
  waiting for transfers between devices: 84.2 us -> 82.4 us
    pallas_call x1 -> x2, Pallas kernels: 24.8 us -> 29.2 us  [the longest x1 25.1 us: factor(): pl.pallas_call(functools.partial(factor_kernel, n, p0, p1, tiles), out_sh...]
    dot_general x1 -> x0, matrix products: 4.15 us -> none  [local_fast(): jnp.dot(hadamard(rows_dev, jnp.bfloat16), flipped, preferred_element_type...]
    ppermute x14, waiting for transfers between devices: 37.9 us -> 36.1 us  [xor_send(): return lax.ppermute(value, AXES, [(d, d ^ mask) for d in range(n_dev)])]
where the time goes in v4:
time: 139 us
  waiting for transfers between devices  82.4 us (59%)
  Pallas kernels  31.1 us (22%)
  starting transfers between devices  22.6 us (16%)
  other arithmetic  2.61 us (2%)
    all_to_all x1, waiting for transfers between devices, local_fast(): lax.all_to_all(local_mix, AXES, split_axis=0, concat_axis=0, tiled=True)  46.3 us
    ppermute x14, waiting for transfers between devices, xor_send(): return lax.ppermute(value, AXES, [(d, d ^ mask) for d in range(n_dev)])  36.1 us
    pallas_call x1, Pallas kernels, factor(): pl.pallas_call(functools.partial(factor_kernel, n, p0, p1, tiles), out_sh...  25.1 us
    ppermute x14, starting transfers between devices, xor_send(): return lax.ppermute(value, AXES, [(d, d ^ mask) for d in range(n_dev)])  15.3 us
    all_to_all x1, starting transfers between devices, local_fast(): lax.all_to_all(local_mix, AXES, split_axis=0, concat_axis=0, tiled=True)  7.33 us
    pallas_call x1, Pallas kernels, local_fast(): pl.pallas_call(local_kernel, grid=(n // width,), out_shape=jax.ShapeDtype...  4.11 us
  transfers between devices with their start and end apart: 15, of which 12 were waited for; matrix products, arithmetic and copies ran while one was open for 2% of the time, Pallas kernels for 0%

profile of v4, /device:TPU:0, one launch (start us, length us, event | category | flops | bytes accessed | tf_op | source)
XLA Modules:
  0.0 139.1 jit_solution(2913101011908867000)
XLA Ops:
  0.0 4.1 %local_mix.1 = f32[512,1024]{1,0:T(8,128)} custom-call(s32[1,512]{1,0:T(1,128)} %bitcast.6, bf16[512,1024]{1,0:T(8,128)(2,1)} %panel_ref.1), custom_call_target="tpu_custom_call" | custom-call | tf_op jit(solution)/shard_map/local_mix/pallas_call | solution.py:434
  4.1 7.3 %all-to-all-start = ((f32[32,16,1024]{2,1,0:T(8,128)}), f32[32,16,1024]{2,1,0:T(8,128)S(1)}, u32[]{:S(2)}, u32[]{:S(2)}) async-start(f32[32,16,1024]{2,1,0:T(8,128)} %bitcast.5), calls=%async_computation | async-start | bytes 4194304 | tf_op jit(solution)/shard_map/all_to_all | solution.py:447
  11.5 2.3 %compare_reduce_fusion = pred[512]{0:T(512)(128)(4,1)S(1)} fusion(s32[8192]{0:T(1024)S(1)} %copy-done, s32[512]{0:T(512)S(1)} %fusion.12), kind=kLoop, calls=%fused_computation | loop fusion | flops 8388096 | bytes 35328 | tf_op jit(solution)/shard_map/reduce_or | solution.py:452
  13.8 46.3 %all-to-all-done.x_ref = f32[32,16,1024]{2,1,0:T(8,128)S(1)} async-done(((f32[32,16,1024]{2,1,0:T(8,128)}), f32[32,16,1024]{2,1,0:T(8,128)S(1)}, u32[]{:S(2)}, u32[]{:S(2)}) %all-to-all-start) | async-done | bytes 2097184 | tf_op jit(solution)/shard_map/all_to_all | solution.py:447
  60.2 1.9 %sketch_gram.1 = (f32[16,8,2176]{2,1,0:T(8,128)S(1)}, f32[16,8,2176]{2,1,0:T(8,128)S(1)}) custom-call(s32[1]{0:T(128)} %bitcast.me_ref, f32[32,16,1024]{2,1,0:T(8,128)S(1)} %all-to-all-done.x_ref, f32[512,128]{1,0:T(8,128)S(1)} %broadcast_in_dim.23.m_ref), custom_call_target="tpu_custom_call" | custom-call | tf_op jit(solution)/shard_map/sketch_gram/pallas_call | solution.py:473
  62.2 2.7 %collective-permute-done = f32[16,8,2176]{2,1,0:T(8,128)S(1)} collective-permute-done((f32[16,8,2176]{2,1,0:T(8,128)S(1)}, f32[16,8,2176]{2,1,0:T(8,128)S(1)}, u32[]{:S(2)}, u32[]{:S(2)}) %collective-permute-start) | collective-permute-done | bytes 1114144 | tf_op jit(solution)/shard_map/ppermute | solution.py:416
  65.1 1.5 %collective-permute-start.1 = (f32[4,8,2176]{2,1,0:T(8,128)S(1)}, f32[4,8,2176]{2,1,0:T(8,128)S(1)}, u32[]{:S(2)}, u32[]{:S(2)}) collective-permute-start(f32[4,8,2176]{2,1,0:T(8,128)S(1)} %get-tuple-element.11), channel_id=1, source_target_pairs={{0,4},{1,5},{2,6},{3,7},{4,0},{5,1},{6,2},{7,3},{8,12},{9,13},{10,... | collective-permute-start | bytes 835592 | tf_op jit(solution)/shard_map/ppermute | solution.py:416
  66.7 1.6 %collective-permute-start.3 = (f32[4,8,2176]{2,1,0:T(8,128)S(1)}, f32[4,8,2176]{2,1,0:T(8,128)S(1)}, u32[]{:S(2)}, u32[]{:S(2)}) collective-permute-start(f32[4,8,2176]{2,1,0:T(8,128)S(1)} %get-tuple-element.12), channel_id=1, source_target_pairs={{0,5},{1,4},{2,7},{3,6},{4,1},{5,0},{6,3},{7,2},{8,13},{9,12},{10,... | collective-permute-start | bytes 835592 | tf_op jit(solution)/shard_map/ppermute | solution.py:416
  68.7 6.0 %collective-permute-done.1 = f32[4,8,2176]{2,1,0:T(8,128)S(1)} collective-permute-done((f32[4,8,2176]{2,1,0:T(8,128)S(1)}, f32[4,8,2176]{2,1,0:T(8,128)S(1)}, u32[]{:S(2)}, u32[]{:S(2)}) %collective-permute-start.1) | collective-permute-done | bytes 278560 | tf_op jit(solution)/shard_map/ppermute | solution.py:416
  74.7 6.3 %collective-permute-done.3 = f32[4,8,2176]{2,1,0:T(8,128)S(1)} collective-permute-done((f32[4,8,2176]{2,1,0:T(8,128)S(1)}, f32[4,8,2176]{2,1,0:T(8,128)S(1)}, u32[]{:S(2)}, u32[]{:S(2)}) %collective-permute-start.3) | collective-permute-done | bytes 278560 | tf_op jit(solution)/shard_map/ppermute | solution.py:416
  81.0 1.4 collective-permute-done.2
  84.1 2.0 %collective-permute-start.5 = (f32[1,8,2176]{2,1,0:T(8,128)S(1)}, f32[1,8,2176]{2,1,0:T(8,128)S(1)}, u32[]{:S(2)}, u32[]{:S(2)}) collective-permute-start(f32[1,8,2176]{2,1,0:T(8,128)S(1)} %get-tuple-element.16), channel_id=1, source_target_pairs={{0,16},{1,17},{2,18},{3,19},{4,20},{5,21},{6,22},{7,23},{8,24},{9,... | collective-permute-start | bytes 208904 | tf_op jit(solution)/shard_map/ppermute | solution.py:416
  86.1 1.3 collective-permute-done.4
  87.4 1.8 %collective-permute-done.6 = f32[1,8,2176]{2,1,0:T(8,128)S(1)} collective-permute-done((f32[1,8,2176]{2,1,0:T(8,128)S(1)}, f32[1,8,2176]{2,1,0:T(8,128)S(1)}, u32[]{:S(2)}, u32[]{:S(2)}) %collective-permute-start.6) | collective-permute-done | bytes 69664 | tf_op jit(solution)/shard_map/ppermute | solution.py:416
  89.2 2.1 %collective-permute-done.5 = f32[1,8,2176]{2,1,0:T(8,128)S(1)} collective-permute-done((f32[1,8,2176]{2,1,0:T(8,128)S(1)}, f32[1,8,2176]{2,1,0:T(8,128)S(1)}, u32[]{:S(2)}, u32[]{:S(2)}) %collective-permute-start.5) | collective-permute-done | bytes 69664 | tf_op jit(solution)/shard_map/ppermute | solution.py:416
  91.3 2.1 %collective-permute-start.9 = (f32[1,8,2176]{2,1,0:T(8,128)S(1)}, f32[1,8,2176]{2,1,0:T(8,128)S(1)}, u32[]{:S(2)}, u32[]{:S(2)}) collective-permute-start(f32[1,8,2176]{2,1,0:T(8,128)S(1)} %get-tuple-element.10), channel_id=1, source_target_pairs={{0,24},{1,25},{2,26},{3,27},{4,28},{5,29},{6,30},{7,31},{8,16},{9,... | collective-permute-start | bytes 208904 | tf_op jit(solution)/shard_map/ppermute | solution.py:416
  93.4 2.3 %collective-permute-start.7 = (f32[1,8,2176]{2,1,0:T(8,128)S(1)}, f32[1,8,2176]{2,1,0:T(8,128)S(1)}, u32[]{:S(2)}, u32[]{:S(2)}) collective-permute-start(f32[1,8,2176]{2,1,0:T(8,128)S(1)} %get-tuple-element.10), channel_id=1, source_target_pairs={{0,8},{1,9},{2,10},{3,11},{4,12},{5,13},{6,14},{7,15},{8,0},{9,1},... | collective-permute-start | bytes 208904 | tf_op jit(solution)/shard_map/ppermute | solution.py:416
  95.8 1.7 %collective-permute-done.9 = f32[1,8,2176]{2,1,0:T(8,128)S(1)} collective-permute-done((f32[1,8,2176]{2,1,0:T(8,128)S(1)}, f32[1,8,2176]{2,1,0:T(8,128)S(1)}, u32[]{:S(2)}, u32[]{:S(2)}) %collective-permute-start.9) | collective-permute-done | bytes 69664 | tf_op jit(solution)/shard_map/ppermute | solution.py:416
  97.5 1.5 %collective-permute-done.8 = f32[1,8,2176]{2,1,0:T(8,128)S(1)} collective-permute-done((f32[1,8,2176]{2,1,0:T(8,128)S(1)}, f32[1,8,2176]{2,1,0:T(8,128)S(1)}, u32[]{:S(2)}, u32[]{:S(2)}) %collective-permute-start.8) | collective-permute-done | bytes 69664 | tf_op jit(solution)/shard_map/ppermute | solution.py:416
  99.0 1.7 %collective-permute-start.12 = (f32[4,8,2176]{2,1,0:T(8,128)S(1)}, f32[4,8,2176]{2,1,0:T(8,128)S(1)}, u32[]{:S(2)}, u32[]{:S(2)}) collective-permute-start(f32[4,8,2176]{2,1,0:T(8,128)S(1)} %pad_maximum_fusion), channel_id=1, source_target_pairs={{0,5},{1,4},{2,7},{3,6},{4,1},{5,0},{6,3},{7,2},{8,13},{9,12},{10,... | collective-permute-start | bytes 835592 | tf_op jit(solution)/shard_map/ppermute | solution.py:416
  100.7 1.2 collective-permute-start.11
  102.6 8.5 %collective-permute-done.10 = f32[4,8,2176]{2,1,0:T(8,128)S(1)} collective-permute-done((f32[4,8,2176]{2,1,0:T(8,128)S(1)}, f32[4,8,2176]{2,1,0:T(8,128)S(1)}, u32[]{:S(2)}, u32[]{:S(2)}) %collective-permute-start.10) | collective-permute-done | bytes 278560 | tf_op jit(solution)/shard_map/ppermute | solution.py:416
  111.4 2.7 %collective-permute-done.13.recv_ref = f32[16,8,2176]{2,1,0:T(8,128)S(1)} collective-permute-done((f32[16,8,2176]{2,1,0:T(8,128)S(1)}, f32[16,8,2176]{2,1,0:T(8,128)S(1)}, u32[]{:S(2)}, u32[]{:S(2)}) %collective-permute-start.13) | collective-permute-done | bytes 1114144 | tf_op jit(solution)/shard_map/ppermute | solution.py:416
  114.0 25.1 %factor.1 = f32[64,512]{1,0:T(8,128)} custom-call(s32[3]{0:T(128)S(1)} %pad_add_fusion.pos_ref, f32[16,8,2176]{2,1,0:T(8,128)S(1)} %constant_dynamic-update-slice_fusion.own_ref, f32[16,8,2176]{2,1,0:T(8,128)S(1)} %collective-permute-done.13.recv_ref), custom_call_target="tpu_custom_call" | custom-call | flops 17179869184 | bytes 1048576 | tf_op jit(solution)/shard_map/factor/pallas_call | solution.py:508
  (28 shorter events, 3.4 us)
Async XLA Ops:
  4.1 7.4 %copy-start = (s32[8192]{0:T(1024)S(1)}, s32[8192]{0:T(1024)}, u32[]{:S(2)}) copy-start(s32[8192]{0:T(1024)} %param.5) | copy-start | bytes 98308
  4.1 56.0 %all-to-all-start = ((f32[32,16,1024]{2,1,0:T(8,128)}), f32[32,16,1024]{2,1,0:T(8,128)S(1)}, u32[]{:S(2)}, u32[]{:S(2)}) async-start(f32[32,16,1024]{2,1,0:T(8,128)} %bitcast.5), calls=%async_computation | async-start | bytes 4194304 | tf_op jit(solution)/shard_map/all_to_all | solution.py:447
  62.1 2.8 %collective-permute-start = (f32[16,8,2176]{2,1,0:T(8,128)S(1)}, f32[16,8,2176]{2,1,0:T(8,128)S(1)}, u32[]{:S(2)}, u32[]{:S(2)}) collective-permute-start(f32[16,8,2176]{2,1,0:T(8,128)S(1)} %get-tuple-element.8), channel_id=1, source_target_pairs={{0,2},{1,3},{2,0},{3,1},{4,6},{5,7},{6,4},{7,5},{8,10},{9,11},{10,... | collective-permute-start | bytes 3342344 | tf_op jit(solution)/shard_map/ppermute | solution.py:416
  65.1 9.6 %collective-permute-start.1 = (f32[4,8,2176]{2,1,0:T(8,128)S(1)}, f32[4,8,2176]{2,1,0:T(8,128)S(1)}, u32[]{:S(2)}, u32[]{:S(2)}) collective-permute-start(f32[4,8,2176]{2,1,0:T(8,128)S(1)} %get-tuple-element.11), channel_id=1, source_target_pairs={{0,4},{1,5},{2,6},{3,7},{4,0},{5,1},{6,2},{7,3},{8,12},{9,13},{10,... | collective-permute-start | bytes 835592 | tf_op jit(solution)/shard_map/ppermute | solution.py:416
  66.7 14.4 %collective-permute-start.3 = (f32[4,8,2176]{2,1,0:T(8,128)S(1)}, f32[4,8,2176]{2,1,0:T(8,128)S(1)}, u32[]{:S(2)}, u32[]{:S(2)}) collective-permute-start(f32[4,8,2176]{2,1,0:T(8,128)S(1)} %get-tuple-element.12), channel_id=1, source_target_pairs={{0,5},{1,4},{2,7},{3,6},{4,1},{5,0},{6,3},{7,2},{8,13},{9,12},{10,... | collective-permute-start | bytes 835592 | tf_op jit(solution)/shard_map/ppermute | solution.py:416
  68.3 14.1 %collective-permute-start.2 = (f32[4,8,2176]{2,1,0:T(8,128)S(1)}, f32[4,8,2176]{2,1,0:T(8,128)S(1)}, u32[]{:S(2)}, u32[]{:S(2)}) collective-permute-start(f32[4,8,2176]{2,1,0:T(8,128)S(1)} %get-tuple-element.13), channel_id=1, source_target_pairs={{0,1},{1,0},{2,3},{3,2},{4,5},{5,4},{6,7},{7,6},{8,9},{9,8},{10,11... | collective-permute-start | bytes 835592 | tf_op jit(solution)/shard_map/ppermute | solution.py:416
  82.5 4.9 %collective-permute-start.4 = (f32[1,8,2176]{2,1,0:T(8,128)S(1)}, f32[1,8,2176]{2,1,0:T(8,128)S(1)}, u32[]{:S(2)}, u32[]{:S(2)}) collective-permute-start(f32[1,8,2176]{2,1,0:T(8,128)S(1)} %get-tuple-element.14), channel_id=1, source_target_pairs={{0,8},{1,9},{2,10},{3,11},{4,12},{5,13},{6,14},{7,15},{8,0},{9,1},... | collective-permute-start | bytes 208904 | tf_op jit(solution)/shard_map/ppermute | solution.py:416
  83.0 6.2 %collective-permute-start.6 = (f32[1,8,2176]{2,1,0:T(8,128)S(1)}, f32[1,8,2176]{2,1,0:T(8,128)S(1)}, u32[]{:S(2)}, u32[]{:S(2)}) collective-permute-start(f32[1,8,2176]{2,1,0:T(8,128)S(1)} %get-tuple-element.15), channel_id=1, source_target_pairs={{0,24},{1,25},{2,26},{3,27},{4,28},{5,29},{6,30},{7,31},{8,16},{9,... | collective-permute-start | bytes 208904 | tf_op jit(solution)/shard_map/ppermute | solution.py:416
  84.1 7.2 %collective-permute-start.5 = (f32[1,8,2176]{2,1,0:T(8,128)S(1)}, f32[1,8,2176]{2,1,0:T(8,128)S(1)}, u32[]{:S(2)}, u32[]{:S(2)}) collective-permute-start(f32[1,8,2176]{2,1,0:T(8,128)S(1)} %get-tuple-element.16), channel_id=1, source_target_pairs={{0,16},{1,17},{2,18},{3,19},{4,20},{5,21},{6,22},{7,23},{8,24},{9,... | collective-permute-start | bytes 208904 | tf_op jit(solution)/shard_map/ppermute | solution.py:416
  91.3 6.2 %collective-permute-start.9 = (f32[1,8,2176]{2,1,0:T(8,128)S(1)}, f32[1,8,2176]{2,1,0:T(8,128)S(1)}, u32[]{:S(2)}, u32[]{:S(2)}) collective-permute-start(f32[1,8,2176]{2,1,0:T(8,128)S(1)} %get-tuple-element.10), channel_id=1, source_target_pairs={{0,24},{1,25},{2,26},{3,27},{4,28},{5,29},{6,30},{7,31},{8,16},{9,... | collective-permute-start | bytes 208904 | tf_op jit(solution)/shard_map/ppermute | solution.py:416
  93.4 5.5 %collective-permute-start.8 = (f32[1,8,2176]{2,1,0:T(8,128)S(1)}, f32[1,8,2176]{2,1,0:T(8,128)S(1)}, u32[]{:S(2)}, u32[]{:S(2)}) collective-permute-start(f32[1,8,2176]{2,1,0:T(8,128)S(1)} %get-tuple-element.10), channel_id=1, source_target_pairs={{0,16},{1,17},{2,18},{3,19},{4,20},{5,21},{6,22},{7,23},{8,24},{9,... | collective-permute-start | bytes 208904 | tf_op jit(solution)/shard_map/ppermute | solution.py:416
  93.4 5.5 %collective-permute-start.7 = (f32[1,8,2176]{2,1,0:T(8,128)S(1)}, f32[1,8,2176]{2,1,0:T(8,128)S(1)}, u32[]{:S(2)}, u32[]{:S(2)}) collective-permute-start(f32[1,8,2176]{2,1,0:T(8,128)S(1)} %get-tuple-element.10), channel_id=1, source_target_pairs={{0,8},{1,9},{2,10},{3,11},{4,12},{5,13},{6,14},{7,15},{8,0},{9,1},... | collective-permute-start | bytes 208904 | tf_op jit(solution)/shard_map/ppermute | solution.py:416
  99.0 12.2 %collective-permute-start.12 = (f32[4,8,2176]{2,1,0:T(8,128)S(1)}, f32[4,8,2176]{2,1,0:T(8,128)S(1)}, u32[]{:S(2)}, u32[]{:S(2)}) collective-permute-start(f32[4,8,2176]{2,1,0:T(8,128)S(1)} %pad_maximum_fusion), channel_id=1, source_target_pairs={{0,5},{1,4},{2,7},{3,6},{4,1},{5,0},{6,3},{7,2},{8,13},{9,12},{10,... | collective-permute-start | bytes 835592 | tf_op jit(solution)/shard_map/ppermute | solution.py:416
  100.7 10.5 %collective-permute-start.11 = (f32[4,8,2176]{2,1,0:T(8,128)S(1)}, f32[4,8,2176]{2,1,0:T(8,128)S(1)}, u32[]{:S(2)}, u32[]{:S(2)}) collective-permute-start(f32[4,8,2176]{2,1,0:T(8,128)S(1)} %pad_maximum_fusion), channel_id=1, source_target_pairs={{0,1},{1,0},{2,3},{3,2},{4,5},{5,4},{6,7},{7,6},{8,9},{9,8},{10,11... | collective-permute-start | bytes 835592 | tf_op jit(solution)/shard_map/ppermute | solution.py:416
  101.9 9.2 %collective-permute-start.10 = (f32[4,8,2176]{2,1,0:T(8,128)S(1)}, f32[4,8,2176]{2,1,0:T(8,128)S(1)}, u32[]{:S(2)}, u32[]{:S(2)}) collective-permute-start(f32[4,8,2176]{2,1,0:T(8,128)S(1)} %pad_maximum_fusion), channel_id=1, source_target_pairs={{0,4},{1,5},{2,6},{3,7},{4,0},{5,1},{6,2},{7,3},{8,12},{9,13},{10,... | collective-permute-start | bytes 835592 | tf_op jit(solution)/shard_map/ppermute | solution.py:416
  111.2 2.8 %collective-permute-start.13 = (f32[16,8,2176]{2,1,0:T(8,128)S(1)}, f32[16,8,2176]{2,1,0:T(8,128)S(1)}, u32[]{:S(2)}, u32[]{:S(2)}) collective-permute-start(f32[16,8,2176]{2,1,0:T(8,128)S(1)} %constant_dynamic-update-slice_fusion.own_ref), channel_id=1, source_target_pairs={{0,2},{1,3},{2,0},{3,1},{4,6},{5,7},{6,4},{7,5},{8,10},{9,11},{10,... | collective-permute-start | bytes 3342344 | tf_op jit(solution)/shard_map/ppermute | solution.py:416

commit v5 on v4

--- a/solution.py
+++ b/solution.py
@@ -164,16 +164,23 @@
     return jnp.concatenate(out, axis=0)
 
 
-def scaled(S, off, other):
+def scales(S, off):
     lane = lax.broadcasted_iota(jnp.int32, S.shape, 1)
     row = lax.broadcasted_iota(jnp.int32, S.shape, 0)
     diag = jnp.where(lane == row + off, S, 0.0)
-    down = lax.rsqrt(jnp.sum(diag, axis=1, keepdims=True))
+    down = jnp.broadcast_to(lax.rsqrt(jnp.sum(diag, axis=1, keepdims=True)), S.shape)
     half = (lane >= off) & (lane < off + S.shape[0])
     across = jnp.where(half[0:1], jnp.sum(diag, axis=0, keepdims=True), 1.0)
     root = lax.rsqrt(across)
-    X = jnp.where(half, S * down * root, jnp.where(lane == row + other, down, 0.0))
-    return X, jnp.where(half[0:1], across * root, 1.0)
+    return down, root, across * root
+
+
+def scaled(S, scale, off, other):
+    down, root, _ = scale
+    lane = lax.broadcasted_iota(jnp.int32, S.shape, 1)
+    row = lax.broadcasted_iota(jnp.int32, S.shape, 0)
+    half = (lane >= off) & (lane < off + S.shape[0])
+    return jnp.where(half, S * (down * root), jnp.where(lane == row + other, down, 0.0))
 
 
 def local_kernel(sign_ref, panel_ref, out_ref, signed):
@@ -347,6 +354,11 @@
         zero = jnp.zeros(value.shape, jnp.bfloat16)
         return [jnp.concatenate([zero, v] if top else [v, zero], axis=0) for v in split(value)]
 
+    def gram_scales(k):
+        tile = diagonal(k)
+        return scales(tile[:H], 0), scales(tile[H:], H)
+
+    upper, lower = gram_scales(p0)
     D = diagonal(p0)
     if p0:
         left = above(p0, slice(p0 * B, (p0 + 1) * B))
@@ -357,7 +369,11 @@
         rest = slice(r + B, n)
         then = slice(r + B, r + 2 * B)
         tail = k < nb - 1
-        X1, back1 = scaled(D[:H], 0, H)
+        X1 = scaled(D[:H], upper, 0, H)
+        back1, back2 = upper[2], lower[2]
+        scale2 = lower
+        if k < p1 - 1:
+            upper, lower = gram_scales(k + 1)
         if tail:
             R = beside(k)
             if k:
@@ -372,7 +388,7 @@
         U1 = mm6(f1, under(D[:H], True), 1, 0)
         u12 = split(jnp.where(low, 0.0, U1))
         D2 = D[H:] - mm6(u12, u12, 0, 0)[H:]
-        X2, back2 = scaled(D2, H, 0)
+        X2 = scaled(D2, scale2, H, 0)
         store(r, here, jnp.where(low, jnp.where(lane >= row, F1, 0.0), U1))
         if tail:
             P1 = mm6(f1, under(R[:H], True), 1, 0)
@@ -430,7 +446,7 @@
 
     vmem = pl.BlockSpec(memory_space=pltpu.VMEM)
     smem = pl.BlockSpec(memory_space=pltpu.SMEM)
-    width = 2 * TILE
+    width = math.gcd(n, 4 * TILE)
     local_mix = pl.pallas_call(
         local_kernel,
         grid=(n // width,),

time: 139 us -> 138 us (level)
  Pallas kernels: 31.1 us -> 29.5 us
where the time goes in v5:
time: 138 us
  waiting for transfers between devices  82.4 us (60%)
  Pallas kernels  29.5 us (21%)
  starting transfers between devices  22.6 us (16%)
  other arithmetic  2.61 us (2%)
    all_to_all x1, waiting for transfers between devices, local_fast(): lax.all_to_all(local_mix, AXES, split_axis=0, concat_axis=0, tiled=True)  46.3 us
    ppermute x14, waiting for transfers between devices, xor_send(): return lax.ppermute(value, AXES, [(d, d ^ mask) for d in range(n_dev)])  36.1 us
    pallas_call x1, Pallas kernels, factor(): pl.pallas_call(functools.partial(factor_kernel, n, p0, p1, tiles), out_sh...  24.9 us
    ppermute x14, starting transfers between devices, xor_send(): return lax.ppermute(value, AXES, [(d, d ^ mask) for d in range(n_dev)])  15.3 us
    all_to_all x1, starting transfers between devices, local_fast(): lax.all_to_all(local_mix, AXES, split_axis=0, concat_axis=0, tiled=True)  7.32 us
    pallas_call x1, Pallas kernels, local_fast(): pl.pallas_call(local_kernel, grid=(n // width,), out_shape=jax.ShapeDtype...  2.76 us
  transfers between devices with their start and end apart: 15, of which 12 were waited for; matrix products, arithmetic and copies ran while one was open for 2% of the time, Pallas kernels for 0%

profile of v5, /device:TPU:0, one launch (start us, length us, event | category | flops | bytes accessed | tf_op | source)
XLA Modules:
  0.0 137.6 jit_solution(18359039183888283809)
XLA Ops:
  0.0 2.8 %local_mix.1 = f32[512,1024]{1,0:T(8,128)} custom-call(s32[1,512]{1,0:T(1,128)} %bitcast.6, bf16[512,1024]{1,0:T(8,128)(2,1)} %panel_ref.1), custom_call_target="tpu_custom_call" | custom-call | tf_op jit(solution)/shard_map/local_mix/pallas_call | solution.py:450
  2.8 7.3 %all-to-all-start = ((f32[32,16,1024]{2,1,0:T(8,128)}), f32[32,16,1024]{2,1,0:T(8,128)S(1)}, u32[]{:S(2)}, u32[]{:S(2)}) async-start(f32[32,16,1024]{2,1,0:T(8,128)} %bitcast.5), calls=%async_computation | async-start | bytes 4194304 | tf_op jit(solution)/shard_map/all_to_all | solution.py:463
  10.2 2.3 %compare_reduce_fusion = pred[512]{0:T(512)(128)(4,1)S(1)} fusion(s32[8192]{0:T(1024)S(1)} %copy-done, s32[512]{0:T(512)S(1)} %fusion.12), kind=kLoop, calls=%fused_computation | loop fusion | flops 8388096 | bytes 35328 | tf_op jit(solution)/shard_map/reduce_or | solution.py:468
  12.5 46.3 %all-to-all-done.x_ref = f32[32,16,1024]{2,1,0:T(8,128)S(1)} async-done(((f32[32,16,1024]{2,1,0:T(8,128)}), f32[32,16,1024]{2,1,0:T(8,128)S(1)}, u32[]{:S(2)}, u32[]{:S(2)}) %all-to-all-start) | async-done | bytes 2097184 | tf_op jit(solution)/shard_map/all_to_all | solution.py:463
  58.9 1.9 %sketch_gram.1 = (f32[16,8,2176]{2,1,0:T(8,128)S(1)}, f32[16,8,2176]{2,1,0:T(8,128)S(1)}) custom-call(s32[1]{0:T(128)} %bitcast.me_ref, f32[32,16,1024]{2,1,0:T(8,128)S(1)} %all-to-all-done.x_ref, f32[512,128]{1,0:T(8,128)S(1)} %broadcast_in_dim.23.m_ref), custom_call_target="tpu_custom_call" | custom-call | tf_op jit(solution)/shard_map/sketch_gram/pallas_call | solution.py:489
  60.9 2.7 %collective-permute-done = f32[16,8,2176]{2,1,0:T(8,128)S(1)} collective-permute-done((f32[16,8,2176]{2,1,0:T(8,128)S(1)}, f32[16,8,2176]{2,1,0:T(8,128)S(1)}, u32[]{:S(2)}, u32[]{:S(2)}) %collective-permute-start) | collective-permute-done | bytes 1114144 | tf_op jit(solution)/shard_map/ppermute | solution.py:432
  63.8 1.5 %collective-permute-start.1 = (f32[4,8,2176]{2,1,0:T(8,128)S(1)}, f32[4,8,2176]{2,1,0:T(8,128)S(1)}, u32[]{:S(2)}, u32[]{:S(2)}) collective-permute-start(f32[4,8,2176]{2,1,0:T(8,128)S(1)} %get-tuple-element.11), channel_id=1, source_target_pairs={{0,4},{1,5},{2,6},{3,7},{4,0},{5,1},{6,2},{7,3},{8,12},{9,13},{10,... | collective-permute-start | bytes 835592 | tf_op jit(solution)/shard_map/ppermute | solution.py:432
  65.3 1.6 %collective-permute-start.3 = (f32[4,8,2176]{2,1,0:T(8,128)S(1)}, f32[4,8,2176]{2,1,0:T(8,128)S(1)}, u32[]{:S(2)}, u32[]{:S(2)}) collective-permute-start(f32[4,8,2176]{2,1,0:T(8,128)S(1)} %get-tuple-element.12), channel_id=1, source_target_pairs={{0,5},{1,4},{2,7},{3,6},{4,1},{5,0},{6,3},{7,2},{8,13},{9,12},{10,... | collective-permute-start | bytes 835592 | tf_op jit(solution)/shard_map/ppermute | solution.py:432
  67.3 6.0 %collective-permute-done.1 = f32[4,8,2176]{2,1,0:T(8,128)S(1)} collective-permute-done((f32[4,8,2176]{2,1,0:T(8,128)S(1)}, f32[4,8,2176]{2,1,0:T(8,128)S(1)}, u32[]{:S(2)}, u32[]{:S(2)}) %collective-permute-start.1) | collective-permute-done | bytes 278560 | tf_op jit(solution)/shard_map/ppermute | solution.py:432
  73.4 6.3 %collective-permute-done.3 = f32[4,8,2176]{2,1,0:T(8,128)S(1)} collective-permute-done((f32[4,8,2176]{2,1,0:T(8,128)S(1)}, f32[4,8,2176]{2,1,0:T(8,128)S(1)}, u32[]{:S(2)}, u32[]{:S(2)}) %collective-permute-start.3) | collective-permute-done | bytes 278560 | tf_op jit(solution)/shard_map/ppermute | solution.py:432
  79.7 1.4 collective-permute-done.2
  82.7 2.0 %collective-permute-start.5 = (f32[1,8,2176]{2,1,0:T(8,128)S(1)}, f32[1,8,2176]{2,1,0:T(8,128)S(1)}, u32[]{:S(2)}, u32[]{:S(2)}) collective-permute-start(f32[1,8,2176]{2,1,0:T(8,128)S(1)} %get-tuple-element.16), channel_id=1, source_target_pairs={{0,16},{1,17},{2,18},{3,19},{4,20},{5,21},{6,22},{7,23},{8,24},{9,... | collective-permute-start | bytes 208904 | tf_op jit(solution)/shard_map/ppermute | solution.py:432
  84.7 1.3 collective-permute-done.4
  86.0 1.8 %collective-permute-done.6 = f32[1,8,2176]{2,1,0:T(8,128)S(1)} collective-permute-done((f32[1,8,2176]{2,1,0:T(8,128)S(1)}, f32[1,8,2176]{2,1,0:T(8,128)S(1)}, u32[]{:S(2)}, u32[]{:S(2)}) %collective-permute-start.6) | collective-permute-done | bytes 69664 | tf_op jit(solution)/shard_map/ppermute | solution.py:432
  87.9 2.1 %collective-permute-done.5 = f32[1,8,2176]{2,1,0:T(8,128)S(1)} collective-permute-done((f32[1,8,2176]{2,1,0:T(8,128)S(1)}, f32[1,8,2176]{2,1,0:T(8,128)S(1)}, u32[]{:S(2)}, u32[]{:S(2)}) %collective-permute-start.5) | collective-permute-done | bytes 69664 | tf_op jit(solution)/shard_map/ppermute | solution.py:432
  90.0 2.1 %collective-permute-start.9 = (f32[1,8,2176]{2,1,0:T(8,128)S(1)}, f32[1,8,2176]{2,1,0:T(8,128)S(1)}, u32[]{:S(2)}, u32[]{:S(2)}) collective-permute-start(f32[1,8,2176]{2,1,0:T(8,128)S(1)} %get-tuple-element.10), channel_id=1, source_target_pairs={{0,24},{1,25},{2,26},{3,27},{4,28},{5,29},{6,30},{7,31},{8,16},{9,... | collective-permute-start | bytes 208904 | tf_op jit(solution)/shard_map/ppermute | solution.py:432
  92.1 2.3 %collective-permute-start.7 = (f32[1,8,2176]{2,1,0:T(8,128)S(1)}, f32[1,8,2176]{2,1,0:T(8,128)S(1)}, u32[]{:S(2)}, u32[]{:S(2)}) collective-permute-start(f32[1,8,2176]{2,1,0:T(8,128)S(1)} %get-tuple-element.10), channel_id=1, source_target_pairs={{0,8},{1,9},{2,10},{3,11},{4,12},{5,13},{6,14},{7,15},{8,0},{9,1},... | collective-permute-start | bytes 208904 | tf_op jit(solution)/shard_map/ppermute | solution.py:432
  94.4 1.7 %collective-permute-done.9 = f32[1,8,2176]{2,1,0:T(8,128)S(1)} collective-permute-done((f32[1,8,2176]{2,1,0:T(8,128)S(1)}, f32[1,8,2176]{2,1,0:T(8,128)S(1)}, u32[]{:S(2)}, u32[]{:S(2)}) %collective-permute-start.9) | collective-permute-done | bytes 69664 | tf_op jit(solution)/shard_map/ppermute | solution.py:432
  96.1 1.5 %collective-permute-done.8 = f32[1,8,2176]{2,1,0:T(8,128)S(1)} collective-permute-done((f32[1,8,2176]{2,1,0:T(8,128)S(1)}, f32[1,8,2176]{2,1,0:T(8,128)S(1)}, u32[]{:S(2)}, u32[]{:S(2)}) %collective-permute-start.8) | collective-permute-done | bytes 69664 | tf_op jit(solution)/shard_map/ppermute | solution.py:432
  97.6 1.7 %collective-permute-start.12 = (f32[4,8,2176]{2,1,0:T(8,128)S(1)}, f32[4,8,2176]{2,1,0:T(8,128)S(1)}, u32[]{:S(2)}, u32[]{:S(2)}) collective-permute-start(f32[4,8,2176]{2,1,0:T(8,128)S(1)} %pad_maximum_fusion), channel_id=1, source_target_pairs={{0,5},{1,4},{2,7},{3,6},{4,1},{5,0},{6,3},{7,2},{8,13},{9,12},{10,... | collective-permute-start | bytes 835592 | tf_op jit(solution)/shard_map/ppermute | solution.py:432
  99.3 1.2 collective-permute-start.11
  101.2 8.5 %collective-permute-done.10 = f32[4,8,2176]{2,1,0:T(8,128)S(1)} collective-permute-done((f32[4,8,2176]{2,1,0:T(8,128)S(1)}, f32[4,8,2176]{2,1,0:T(8,128)S(1)}, u32[]{:S(2)}, u32[]{:S(2)}) %collective-permute-start.10) | collective-permute-done | bytes 278560 | tf_op jit(solution)/shard_map/ppermute | solution.py:432
  110.0 2.7 %collective-permute-done.13.recv_ref = f32[16,8,2176]{2,1,0:T(8,128)S(1)} collective-permute-done((f32[16,8,2176]{2,1,0:T(8,128)S(1)}, f32[16,8,2176]{2,1,0:T(8,128)S(1)}, u32[]{:S(2)}, u32[]{:S(2)}) %collective-permute-start.13) | collective-permute-done | bytes 1114144 | tf_op jit(solution)/shard_map/ppermute | solution.py:432
  112.7 24.9 %factor.1 = f32[64,512]{1,0:T(8,128)} custom-call(s32[3]{0:T(128)S(1)} %pad_add_fusion.pos_ref, f32[16,8,2176]{2,1,0:T(8,128)S(1)} %constant_dynamic-update-slice_fusion.own_ref, f32[16,8,2176]{2,1,0:T(8,128)S(1)} %collective-permute-done.13.recv_ref), custom_call_target="tpu_custom_call" | custom-call | flops 17179869184 | bytes 1048576 | tf_op jit(solution)/shard_map/factor/pallas_call | solution.py:524
  (28 shorter events, 3.4 us)
Async XLA Ops:
  2.8 7.4 %copy-start = (s32[8192]{0:T(1024)S(1)}, s32[8192]{0:T(1024)}, u32[]{:S(2)}) copy-start(s32[8192]{0:T(1024)} %param.5) | copy-start | bytes 98308
  2.8 56.0 %all-to-all-start = ((f32[32,16,1024]{2,1,0:T(8,128)}), f32[32,16,1024]{2,1,0:T(8,128)S(1)}, u32[]{:S(2)}, u32[]{:S(2)}) async-start(f32[32,16,1024]{2,1,0:T(8,128)} %bitcast.5), calls=%async_computation | async-start | bytes 4194304 | tf_op jit(solution)/shard_map/all_to_all | solution.py:463
  60.8 2.8 %collective-permute-start = (f32[16,8,2176]{2,1,0:T(8,128)S(1)}, f32[16,8,2176]{2,1,0:T(8,128)S(1)}, u32[]{:S(2)}, u32[]{:S(2)}) collective-permute-start(f32[16,8,2176]{2,1,0:T(8,128)S(1)} %get-tuple-element.8), channel_id=1, source_target_pairs={{0,2},{1,3},{2,0},{3,1},{4,6},{5,7},{6,4},{7,5},{8,10},{9,11},{10,... | collective-permute-start | bytes 3342344 | tf_op jit(solution)/shard_map/ppermute | solution.py:432
  63.8 9.6 %collective-permute-start.1 = (f32[4,8,2176]{2,1,0:T(8,128)S(1)}, f32[4,8,2176]{2,1,0:T(8,128)S(1)}, u32[]{:S(2)}, u32[]{:S(2)}) collective-permute-start(f32[4,8,2176]{2,1,0:T(8,128)S(1)} %get-tuple-element.11), channel_id=1, source_target_pairs={{0,4},{1,5},{2,6},{3,7},{4,0},{5,1},{6,2},{7,3},{8,12},{9,13},{10,... | collective-permute-start | bytes 835592 | tf_op jit(solution)/shard_map/ppermute | solution.py:432
  65.3 14.4 %collective-permute-start.3 = (f32[4,8,2176]{2,1,0:T(8,128)S(1)}, f32[4,8,2176]{2,1,0:T(8,128)S(1)}, u32[]{:S(2)}, u32[]{:S(2)}) collective-permute-start(f32[4,8,2176]{2,1,0:T(8,128)S(1)} %get-tuple-element.12), channel_id=1, source_target_pairs={{0,5},{1,4},{2,7},{3,6},{4,1},{5,0},{6,3},{7,2},{8,13},{9,12},{10,... | collective-permute-start | bytes 835592 | tf_op jit(solution)/shard_map/ppermute | solution.py:432
  66.9 14.1 %collective-permute-start.2 = (f32[4,8,2176]{2,1,0:T(8,128)S(1)}, f32[4,8,2176]{2,1,0:T(8,128)S(1)}, u32[]{:S(2)}, u32[]{:S(2)}) collective-permute-start(f32[4,8,2176]{2,1,0:T(8,128)S(1)} %get-tuple-element.13), channel_id=1, source_target_pairs={{0,1},{1,0},{2,3},{3,2},{4,5},{5,4},{6,7},{7,6},{8,9},{9,8},{10,11... | collective-permute-start | bytes 835592 | tf_op jit(solution)/shard_map/ppermute | solution.py:432
  81.2 4.9 %collective-permute-start.4 = (f32[1,8,2176]{2,1,0:T(8,128)S(1)}, f32[1,8,2176]{2,1,0:T(8,128)S(1)}, u32[]{:S(2)}, u32[]{:S(2)}) collective-permute-start(f32[1,8,2176]{2,1,0:T(8,128)S(1)} %get-tuple-element.14), channel_id=1, source_target_pairs={{0,8},{1,9},{2,10},{3,11},{4,12},{5,13},{6,14},{7,15},{8,0},{9,1},... | collective-permute-start | bytes 208904 | tf_op jit(solution)/shard_map/ppermute | solution.py:432
  81.7 6.2 %collective-permute-start.6 = (f32[1,8,2176]{2,1,0:T(8,128)S(1)}, f32[1,8,2176]{2,1,0:T(8,128)S(1)}, u32[]{:S(2)}, u32[]{:S(2)}) collective-permute-start(f32[1,8,2176]{2,1,0:T(8,128)S(1)} %get-tuple-element.15), channel_id=1, source_target_pairs={{0,24},{1,25},{2,26},{3,27},{4,28},{5,29},{6,30},{7,31},{8,16},{9,... | collective-permute-start | bytes 208904 | tf_op jit(solution)/shard_map/ppermute | solution.py:432
  82.7 7.2 %collective-permute-start.5 = (f32[1,8,2176]{2,1,0:T(8,128)S(1)}, f32[1,8,2176]{2,1,0:T(8,128)S(1)}, u32[]{:S(2)}, u32[]{:S(2)}) collective-permute-start(f32[1,8,2176]{2,1,0:T(8,128)S(1)} %get-tuple-element.16), channel_id=1, source_target_pairs={{0,16},{1,17},{2,18},{3,19},{4,20},{5,21},{6,22},{7,23},{8,24},{9,... | collective-permute-start | bytes 208904 | tf_op jit(solution)/shard_map/ppermute | solution.py:432
  90.0 6.2 %collective-permute-start.9 = (f32[1,8,2176]{2,1,0:T(8,128)S(1)}, f32[1,8,2176]{2,1,0:T(8,128)S(1)}, u32[]{:S(2)}, u32[]{:S(2)}) collective-permute-start(f32[1,8,2176]{2,1,0:T(8,128)S(1)} %get-tuple-element.10), channel_id=1, source_target_pairs={{0,24},{1,25},{2,26},{3,27},{4,28},{5,29},{6,30},{7,31},{8,16},{9,... | collective-permute-start | bytes 208904 | tf_op jit(solution)/shard_map/ppermute | solution.py:432
  92.1 5.5 %collective-permute-start.8 = (f32[1,8,2176]{2,1,0:T(8,128)S(1)}, f32[1,8,2176]{2,1,0:T(8,128)S(1)}, u32[]{:S(2)}, u32[]{:S(2)}) collective-permute-start(f32[1,8,2176]{2,1,0:T(8,128)S(1)} %get-tuple-element.10), channel_id=1, source_target_pairs={{0,16},{1,17},{2,18},{3,19},{4,20},{5,21},{6,22},{7,23},{8,24},{9,... | collective-permute-start | bytes 208904 | tf_op jit(solution)/shard_map/ppermute | solution.py:432
  92.1 5.5 %collective-permute-start.7 = (f32[1,8,2176]{2,1,0:T(8,128)S(1)}, f32[1,8,2176]{2,1,0:T(8,128)S(1)}, u32[]{:S(2)}, u32[]{:S(2)}) collective-permute-start(f32[1,8,2176]{2,1,0:T(8,128)S(1)} %get-tuple-element.10), channel_id=1, source_target_pairs={{0,8},{1,9},{2,10},{3,11},{4,12},{5,13},{6,14},{7,15},{8,0},{9,1},... | collective-permute-start | bytes 208904 | tf_op jit(solution)/shard_map/ppermute | solution.py:432
  97.6 12.2 %collective-permute-start.12 = (f32[4,8,2176]{2,1,0:T(8,128)S(1)}, f32[4,8,2176]{2,1,0:T(8,128)S(1)}, u32[]{:S(2)}, u32[]{:S(2)}) collective-permute-start(f32[4,8,2176]{2,1,0:T(8,128)S(1)} %pad_maximum_fusion), channel_id=1, source_target_pairs={{0,5},{1,4},{2,7},{3,6},{4,1},{5,0},{6,3},{7,2},{8,13},{9,12},{10,... | collective-permute-start | bytes 835592 | tf_op jit(solution)/shard_map/ppermute | solution.py:432
  99.3 10.5 %collective-permute-start.11 = (f32[4,8,2176]{2,1,0:T(8,128)S(1)}, f32[4,8,2176]{2,1,0:T(8,128)S(1)}, u32[]{:S(2)}, u32[]{:S(2)}) collective-permute-start(f32[4,8,2176]{2,1,0:T(8,128)S(1)} %pad_maximum_fusion), channel_id=1, source_target_pairs={{0,1},{1,0},{2,3},{3,2},{4,5},{5,4},{6,7},{7,6},{8,9},{9,8},{10,11... | collective-permute-start | bytes 835592 | tf_op jit(solution)/shard_map/ppermute | solution.py:432
  100.6 9.2 %collective-permute-start.10 = (f32[4,8,2176]{2,1,0:T(8,128)S(1)}, f32[4,8,2176]{2,1,0:T(8,128)S(1)}, u32[]{:S(2)}, u32[]{:S(2)}) collective-permute-start(f32[4,8,2176]{2,1,0:T(8,128)S(1)} %pad_maximum_fusion), channel_id=1, source_target_pairs={{0,4},{1,5},{2,6},{3,7},{4,0},{5,1},{6,2},{7,3},{8,12},{9,13},{10,... | collective-permute-start | bytes 835592 | tf_op jit(solution)/shard_map/ppermute | solution.py:432
  109.9 2.8 %collective-permute-start.13 = (f32[16,8,2176]{2,1,0:T(8,128)S(1)}, f32[16,8,2176]{2,1,0:T(8,128)S(1)}, u32[]{:S(2)}, u32[]{:S(2)}) collective-permute-start(f32[16,8,2176]{2,1,0:T(8,128)S(1)} %constant_dynamic-update-slice_fusion.own_ref), channel_id=1, source_target_pairs={{0,2},{1,3},{2,0},{3,1},{4,6},{5,7},{6,4},{7,5},{8,10},{9,11},{10,... | collective-permute-start | bytes 3342344 | tf_op jit(solution)/shard_map/ppermute | solution.py:432
